TPU v7x, 32 devices: a whole 2x2x4 slice. The times are simulated.
32 devices in a mesh: parts: 2 (over y), bank: 4 (over z), tm: 2 (over x), rate: 2 (over core).
Axes of the slice: x: 2, y: 2, z: 4, core: 2. Of those that a mesh axis runs over, the one named last changes fastest.
Arguments:
- strain: float32 [2, 16384], P('rate', ('parts', 'bank', 'tm')), parts along dimension 1, may hold values from -6 to 6
- gate_mask: int32 [16384], P(('parts', 'bank', 'tm')), parts along dimension 0, may hold values 0 or 1
- psd_reset: int32 [16], P(('parts', 'bank', 'tm')), parts along dimension 0, may hold values from 0 to 1
- psd_ref: float32 [2, 512], P('rate'), may hold values from 0.1 to 10
- psd_rate: float32 [2, 512], P('rate'), may hold values from 0.025 to 0.5
- filters: bfloat16 [4, 2, 32, 2048], P('bank', 'rate'), may hold values from -0.125 to 0.125
- basis_count: int32 [4], P('bank'), may hold values from 16 to 32, as said below
- mixing: bfloat16 [4, 2, 4, 2, 32], P('bank', 'rate'), may hold values from -0.75 to 0.75
- autocorrelation: float32 [4, 2, 257], replicated, may hold values from -1.2 to 1.2
Outputs:
- snr_sq: float32 [4, 4, 16384], P(None, 'rate', ('parts', 'bank', 'tm')), parts along dimension 2
- chisq: float32 [4, 4, 16384], P(None, 'rate', ('parts', 'bank', 'tm')), parts along dimension 2
There are 2 independent parts, one for each index of `parts`. A program takes and returns all parts, laid end to end along the dimension named above; an argument that names none is the same for every part. Nothing has to cross between parts.
Inputs may be any that keep to these rules, and one draw needn't show every extreme that they name: `basis_count`: some bank uses all 32 basis filters and another only half of them.
All inputs are finite; a program needn't handle non-finite values. No bound on the sum of `gate_mask` on one device may be relied on, other than what follows from the above.
Results may differ from a plain program's by a relative error of at most 0.0044.
Values may be sent and summed in bfloat16 or wider, within the bound.
No kernel may reach another device: no remote copies, remote signals or barrier semaphores. Data moves between devices by JAX's collectives and lax.ppermute only.
A program may use at most 128 MiB of HBM per device.

v0:
```python
import math

import jax
import jax.numpy as jnp
from jax import lax
from jax.sharding import PartitionSpec as P

HIGHEST = lax.Precision.HIGHEST


def entering(part, axis, combine, identity):
    place = lax.axis_index(axis)
    gathered = jax.tree.map(lambda a: lax.all_gather(a, axis), part)
    state = jax.tree.map(lambda a, e: jnp.zeros_like(a) + jnp.asarray(e, a.dtype), part, identity)

    def one(hop, state):
        return combine(
            state, jax.tree.map(lambda a: lax.dynamic_index_in_dim(a, hop, 0, False), gathered)
        )

    return lax.fori_loop(0, place, one, state)


def from_behind(block, axis, distance):
    devices = range(lax.axis_size(axis))
    route = [((i - distance) % len(devices), i) for i in devices]
    return lax.ppermute(block, axis, route)


def extended_2(block, sides, width):
    for axis, dim in sides:
        count = lax.axis_size(axis)
        forward = [(i, i + 1) for i in range(count - 1)]
        backward = [(target, source) for source, target in forward]
        low = lax.ppermute(
            lax.slice_in_dim(block, block.shape[dim] - width, None, axis=dim), axis, forward
        )
        high = lax.ppermute(lax.slice_in_dim(block, 0, width, axis=dim), axis, backward)
        block = jnp.concatenate([low, block, high], axis=dim)
    return block


def dft_tables(length):
    bin_count = length // 2
    sample = jnp.arange(length, dtype=jnp.int32)
    frequency = jnp.arange(bin_count, dtype=jnp.int32)
    phase_index = sample[:, None] * frequency[None, :] % length
    angle_value = phase_index.astype(jnp.float32) * (2.0 * math.pi / length)
    weights = jnp.where(frequency == 0, 1.0 / length, 2.0 / length).astype(jnp.float32)
    return (jnp.cos(angle_value), jnp.sin(angle_value), weights)


def combine_decay(earlier_map, later_map):
    return (earlier_map[0] * later_map[0], later_map[0] * earlier_map[1] + later_map[1])


def toeplitz_basis(context, taps_bank):
    row_count, context_len = context.shape
    piece_len = context_len // 3
    frame_len = min(128, piece_len)
    basis_num, tap_count = taps_bank.shape
    lag_count = tap_count // frame_len + 1
    line_len = tap_count + 2 * frame_len
    spread = jnp.concatenate(
        [
            jnp.zeros((basis_num, frame_len), taps_bank.dtype),
            taps_bank,
            jnp.zeros((basis_num, frame_len + 1), taps_bank.dtype),
        ],
        axis=1,
    )
    tiled = jnp.tile(spread, (1, frame_len))[:, : frame_len * line_len]
    shifted = tiled.reshape(basis_num, frame_len, line_len)
    table = shifted[:, :, frame_len : frame_len + lag_count * frame_len].reshape(
        basis_num, frame_len, lag_count, frame_len
    )
    first_out = 2 * piece_len // frame_len
    out_frames = piece_len // frame_len
    framed = context.reshape(row_count, context_len // frame_len, frame_len)
    stacked = jnp.stack(
        [framed[:, first_out - lag : first_out - lag + out_frames, :] for lag in range(lag_count)],
        axis=1,
    )
    outputs = jnp.einsum("brfm,imrq->bifq", stacked, table, preferred_element_type=jnp.float32)
    return outputs.reshape(row_count, basis_num, piece_len)


def band_matrix(series, window):
    lead_shape = series.shape[:-1]
    padded = jnp.concatenate([series, jnp.zeros(lead_shape + (window,), series.dtype)], axis=-1)
    tiled = jnp.tile(padded, (1,) * len(lead_shape) + (window,))[..., : window * 3 * window]
    return tiled.reshape(lead_shape + (window, 3 * window))


def chi_square(extended, autocorrelation, window):
    bank_count = extended.shape[0]
    item_count = extended.shape[1]
    total_len = extended.shape[3]
    piece_len = total_len - 2 * window
    frames = piece_len // window
    framed = extended.reshape(bank_count, item_count, 2, frames + 2, window)
    triple = jnp.concatenate(
        [framed[..., 0:frames, :], framed[..., 1 : frames + 1, :], framed[..., 2 : frames + 2, :]],
        axis=-1,
    )
    band_mats = band_matrix(autocorrelation, window)
    folded = jnp.einsum("bmpnk,bdqk->bmpdnq", triple, band_mats, precision=HIGHEST)
    corr_real = folded[:, :, 0, 0] + folded[:, :, 1, 1]
    corr_imag = folded[:, :, 1, 0] - folded[:, :, 0, 1]
    power_ext = extended[:, :, 0] * extended[:, :, 0] + extended[:, :, 1] * extended[:, :, 1]
    power_framed = power_ext.reshape(bank_count, item_count, frames + 2, window)
    power_triple = jnp.concatenate(
        [
            power_framed[..., 0:frames, :],
            power_framed[..., 1 : frames + 1, :],
            power_framed[..., 2 : frames + 2, :],
        ],
        axis=-1,
    )
    ones_band = band_matrix(jnp.ones((1, 2 * window + 1), jnp.float32), window)[0]
    window_sum = jnp.einsum("bmnk,qk->bmnq", power_triple, ones_band, precision=HIGHEST)
    centre = extended[..., window : window + piece_len].reshape(
        bank_count, item_count, 2, frames, window
    )
    energy = centre[:, :, 0] * centre[:, :, 0] + centre[:, :, 1] * centre[:, :, 1]
    lag_energy = jnp.sum(autocorrelation * autocorrelation, axis=(1, 2))
    cross = centre[:, :, 0] * corr_real + centre[:, :, 1] * corr_imag
    chisq = (window_sum - 2.0 * cross + energy * lag_energy[:, None, None, None]) / (2 * window + 1)
    return (
        energy.reshape(bank_count, item_count, piece_len),
        chisq.reshape(bank_count, item_count, piece_len),
    )


def body(
    strain, gate_mask, psd_reset, psd_ref, psd_rate, filters, basis_count, mixing, autocorrelation
):
    piece_len = strain.shape[1]
    cos_table, sin_table, weights = dft_tables(piece_len)
    signal = strain[0] * gate_mask.astype(jnp.float32)
    real_part = jnp.dot(signal, cos_table, precision=HIGHEST)
    imag_part = jnp.dot(signal, sin_table, precision=HIGHEST)
    reference_psd = psd_ref[0]
    decay_rate = psd_rate[0]
    log_power = jnp.log(
        (real_part * real_part + imag_part * imag_part) / (piece_len / 2) + 0.1 * reference_psd
    )
    keep_factor = (1.0 - decay_rate) * (1.0 - 0.5 * psd_reset[0].astype(jnp.float32))
    drive_term = decay_rate * log_power
    prior_keep, prior_drive = entering(
        (keep_factor, drive_term),
        ("bank", "tm"),
        combine_decay,
        (jnp.ones_like(keep_factor), jnp.zeros_like(drive_term)),
    )
    log_psd = keep_factor * (prior_keep * jnp.log(reference_psd) + prior_drive) + drive_term
    bin_scale = jnp.exp(-0.5 * log_psd) * weights
    whitened = jnp.dot(cos_table, real_part * bin_scale, precision=HIGHEST) + jnp.dot(
        sin_table, imag_part * bin_scale, precision=HIGHEST
    )
    own_row = whitened.astype(jnp.bfloat16).reshape(1, piece_len)
    gathered = lax.all_gather(own_row, "bank", axis=0, tiled=True)
    at_start = lax.axis_index("tm") == 0
    earlier = gathered
    previous = []
    for hop_count in range(2):
        moved_rows = from_behind(earlier, "tm", 1)
        rolled = jnp.concatenate([jnp.zeros_like(moved_rows[:1]), moved_rows[:-1]], axis=0)
        earlier = jnp.where(at_start, rolled, moved_rows)
        previous.append(earlier)
    context = jnp.concatenate([previous[1], previous[0], gathered], axis=1)
    basis_out = toeplitz_basis(context, filters[0, 0])
    live_basis = (jnp.arange(basis_out.shape[1], dtype=jnp.int32) < basis_count[0]).astype(
        jnp.float32
    )
    basis_rounded = (basis_out * live_basis[None, :, None]).astype(jnp.bfloat16)
    mixing_local = mixing[0, 0]
    templ_total = mixing_local.shape[0]
    share_count = templ_total // lax.axis_size("rate")
    window = autocorrelation.shape[2] // 2
    all_basis, all_mixing = (
        lax.all_gather(basis_rounded[None], "rate", axis=0, tiled=True),
        lax.all_gather(mixing, "rate", axis=1, tiled=True),
    )
    row_start = lax.axis_index("rate") * share_count
    own_mixing = lax.dynamic_slice_in_dim(all_mixing[0], row_start, share_count, 1)
    snr_part = jnp.einsum(
        "cmpi,cbit->mpbt", own_mixing, all_basis, preferred_element_type=jnp.float32
    )
    received = lax.all_to_all(snr_part[None], "bank", split_axis=3, concat_axis=0, tiled=True)
    shaped = received.reshape(received.shape[0], received.shape[1], 2, received.shape[4])
    extended = extended_2(shaped, ((("bank", "tm"), 3),), window)
    snr_sq, chisq = chi_square(extended, autocorrelation, window)
    return (snr_sq, chisq)


def solution(mesh):
    return jax.shard_map(
        body,
        mesh=mesh,
        in_specs=(
            P("rate", ("parts", "bank", "tm")),
            P(("parts", "bank", "tm")),
            P(("parts", "bank", "tm")),
            P("rate", None),
            P("rate", None),
            P("bank", "rate", None, None),
            P("bank"),
            P("bank", "rate", None, None, None),
            P(),
        ),
        out_specs=(
            P(None, "rate", ("parts", "bank", "tm")),
            P(None, "rate", ("parts", "bank", "tm")),
        ),
        check_vma=False,
    )
```

profile of v0, /device:TPU:0, one launch (start us, length us, event | category | flops | bytes accessed | tf_op | source)
XLA Modules:
  0.0 248.0 jit_solution(3940699285153602173)
XLA Ops:
  0.6 0.7 convert_multiply_fusion
  1.3 8.7 %fusion.17 = f32[1,512]{1,0:T(1,128)S(1)} fusion(f32[1024,1]{0,1:T(1,128)S(1)} %bitcast.279), kind=kOutput, calls=%fused_computation.23 | convolution fusion | flops 13631488 | bytes 6144 | tf_op jit(solution)/shard_map/dot_general | solution.py:141
  10.0 0.0 copy-start.2
  10.1 8.8 %fusion.21 = f32[1,512]{1,0:T(1,128)S(1)} fusion(f32[1024,1]{0,1:T(1,128)S(1)} %bitcast.280), kind=kOutput, calls=%fused_computation.25 | convolution fusion | flops 13631488 | bytes 6144 | tf_op jit(solution)/shard_map/dot_general | solution.py:142
  19.6 27.9 %all-gather.2 = f32[8,1,512]{2,1,0:T(1,128)S(1)} all-gather(f32[1,1,512]{2,1,0:T(1,128)S(1)} %multiply_bitcast_fusion), channel_id=1, replica_groups=mesh['parts'=2,'bank'=4,'tm'=2,'rate'=2] {'bank','tm'}, dimensions={0}, use_global_device_ids=true | all-gather | bytes 18432 | tf_op jit(solution)/shard_map/all_gather | solution.py:13
  47.5 26.1 %all-gather.3 = f32[8,1,512]{2,1,0:T(1,128)S(1)} all-gather(f32[1,1,512]{2,1,0:T(1,128)S(1)} %bitcast.269), channel_id=2, replica_groups=mesh['parts'=2,'bank'=4,'tm'=2,'rate'=2] {'bank','tm'}, dimensions={0}, use_global_device_ids=true | all-gather | bytes 18432 | tf_op jit(solution)/shard_map/all_gather | solution.py:13
  73.6 0.2 while.12
  73.9 10.4 %fusion.15 = f32[1,1024]{1,0:T(1,128)S(1)} fusion(f32[512,1]{0,1:T(1,128)S(1)} %bitcast.284), kind=kOutput, calls=%fused_computation.22 | convolution fusion | flops 13631488 | bytes 6144 | tf_op jit(solution)/shard_map/dot_general | solution.py:158
  84.2 0.0 copy-start.3
  84.2 0.0 copy-start
  84.3 10.4 %fusion.19 = f32[1,1024]{1,0:T(1,128)S(1)} fusion(f32[512,1]{0,1:T(1,128)S(1)} %bitcast.283), kind=kOutput, calls=%fused_computation.24 | convolution fusion | flops 13631488 | bytes 6144 | tf_op jit(solution)/shard_map/dot_general | solution.py:158
  94.7 11.9 %all-gather.1 = bf16[4096]{0:T(1024)(128)(2,1)S(1)} all-gather(bf16[1024]{0:T(1024)(128)(2,1)S(1)} %add_convert_fusion), channel_id=3, replica_groups=mesh['parts'=2,'bank'=4,'tm'=2,'rate'=2] {'bank'}, dimensions={0}, use_global_device_ids=true | all-gather | bytes 10240 | tf_op jit(solution)/shard_map/all_gather | solution.py:162
  106.6 0.1 collective-permute-start
  106.8 1.8 all_gather.19
  108.7 0.5 tile.29
  109.2 0.5 slice_reduce_fusion
  110.4 2.0 collective-permute-start.1
  112.5 6.9 %tile.12 = bf16[32,128,2305]{2,1,0:T(8,128)(2,1)} broadcast(bf16[32,2305]{1,0:T(8,128)(2,1)S(1)} %maximum_maximum_fusion), dimensions={0,2} | broadcast | bytes 19030080 | tf_op jit(solution)/shard_map/tile | solution.py:72
  119.4 44.8 %tile.13 = bf16[32,295040]{1,0:T(8,128)(2,1)} reshape(bf16[32,128,2305]{2,1,0:T(8,128)(2,1)} %tile.12) | data formatting | bytes 37765120 | tf_op jit(solution)/shard_map/tile | solution.py:72
  164.2 6.4 %slice-done = bf16[32,294912]{1,0:T(8,128)(2,1)S(1)} async-done(((bf16[32,295040]{1,0:T(8,128)(2,1)}), bf16[32,294912]{1,0:T(8,128)(2,1)S(1)}, s32[]{:S(2)}) %slice-start) | async-done | bytes 18874392 | tf_op jit(solution)/shard_map/slice | solution.py:72
  170.6 9.7 %copy.103 = bf16[4,8,128,2304]{3,2,1,0:T(8,128)(2,1)S(1)} copy(bf16[4,8,128,2304]{3,1,2,0:T(8,128)(2,1)S(1)} %bitcast.240) | data formatting | bytes 37748736
  180.2 7.0 %slice.163 = bf16[32,128,2176]{2,1,0:T(8,128)(2,1)} slice(bf16[32,128,2304]{2,1,0:T(8,128)(2,1)S(1)} %bitcast.241), slice={[0:32], [0:128], [128:2304]} | slice | bytes 35651584 | tf_op jit(solution)/shard_map/slice | solution.py:74
  187.2 22.1 %copy.100 = bf16[32,128,2176]{1,2,0:T(8,128)(2,1)} copy(bf16[32,128,2176]{2,1,0:T(8,128)(2,1)} %slice.163) | data formatting | bytes 35651584
  209.4 0.3 tile.30
  209.7 3.6 %tile.31 = f32[4,2,49280]{2,1,0:T(2,128)} reshape(f32[4,2,128,385]{3,2,1,0:T(8,128)S(1)} %tile.30) | data formatting | bytes 3153920 | tf_op jit(solution)/shard_map/tile | solution.py:91
  213.2 1.4 slice-done.1
  214.6 1.4 reshape.119
  216.0 0.0 collective-permute-done.1
  216.4 8.8 %convolution_bitcast_fusion = f32[4,32,8,128]{3,2,0,1:T(8,128)S(1)} fusion(bf16[32,128,17,128,1]{1,3,2,4,0:T(8,128)(2,1)} %bitcast.239, bf16[4,17,8,128]{3,2,1,0:T(8,128)(2,1)S(1)} %constant_dynamic-update-slice_fusion), kind=kOutput, calls=%fused_computation.14 | convolution fusion | flops 570425344 | bytes 18489344 | tf_op jit(solution)/shard_map/brfm,imrq->bifq/dot_general | solution.py:84
  225.2 0.2 reshape.92
  225.4 0.3 fusion.24
  225.7 2.2 all_gather.24
  227.9 0.3 convolution_bitcast_fusion.1
  228.2 0.6 copy.84
  228.8 3.3 %all-to-all-start = ((f32[1,2,2,4,1024]{4,2,1,0,3:T(2,128)}), f32[1,2,2,4,1024]{4,2,1,0,3:T(2,128)S(1)}, u32[]{:S(2)}, u32[]{:S(2)}) async-start(f32[1,2,2,4,1024]{4,2,1,0,3:T(2,128)} %copy.84), calls=%async_computation | async-start | bytes 131072 | tf_op jit(solution)/shard_map/all_to_all | solution.py:190
  232.1 0.1 multiply_reduce_fusion
  232.2 5.6 %all-to-all-done = f32[1,2,2,4,1024]{4,2,1,0,3:T(2,128)S(1)} async-done(((f32[1,2,2,4,1024]{4,2,1,0,3:T(2,128)}), f32[1,2,2,4,1024]{4,2,1,0,3:T(2,128)S(1)}, u32[]{:S(2)}, u32[]{:S(2)}) %all-to-all-start) | async-done | bytes 65568 | tf_op jit(solution)/shard_map/all_to_all | solution.py:190
  237.8 0.1 reshape.121
  237.8 1.3 collective-permute-start.3
  239.1 4.5 %collective-permute-start.2 = (f32[4,2,2,128]{3,2,1,0:T(2,128)S(1)}, f32[4,2,2,128]{3,2,1,0:T(2,128)S(1)}, u32[]{:S(2)}, u32[]{:S(2)}) collective-permute-start(f32[4,2,2,128]{3,2,1,0:T(2,128)S(1)} %get-tuple-element.62), channel_id=1, source_target_pairs={{0,2},{2,4},{4,6},{6,8},{8,10},{10,12},{12,14},{1,3},{3,5},{5,7},{... | collective-permute-start | bytes 24584 | tf_op jit(solution)/shard_map/ppermute | solution.py:35
  243.7 0.6 add.87
  244.4 0.0 collective-permute-done.3
  244.4 0.7 collective-permute-done.2
  245.1 0.2 fusion.34
  245.3 0.1 reshape.95
  245.4 1.6 fusion.8
  247.0 0.4 fusion.12
  247.4 0.6 reshape.96
  (61 shorter events, 0.6 us)
Async XLA Ops:
  10.0 8.8 %copy-start.4 = (f32[1,512]{1,0:T(1,128)S(1)}, f32[1,512]{1,0:T(1,128)}, u32[]{:S(2)}) copy-start(f32[1,512]{1,0:T(1,128)} %param.14) | copy-start | bytes 6148
  10.0 9.5 %copy-start.2 = (f32[1,512]{1,0:T(1,128)S(1)}, f32[1,512]{1,0:T(1,128)}, u32[]{:S(2)}) copy-start(f32[1,512]{1,0:T(1,128)} %param.15) | copy-start | bytes 6148
  84.2 22.5 %copy-start.5 = (bf16[1,1,4,2,32]{4,3,2,1,0:T(2,128)(2,1)S(1)}, bf16[1,1,4,2,32]{4,3,2,1,0:T(2,128)(2,1)}, u32[]{:S(2)}) copy-start(bf16[1,1,4,2,32]{4,3,2,1,0:T(2,128)(2,1)} %param.18) | copy-start | bytes 1540
  84.2 24.4 %copy-start.3 = (f32[385]{0:T(512)S(1)}, f32[385]{0:T(512)}, u32[]{:S(2)}) copy-start(f32[385]{0:T(512)} %constant.76.clone.1) | copy-start | bytes 4624
  84.2 25.4 %copy-start = (bf16[1,1,32,2048]{3,2,1,0:T(8,128)(2,1)S(1)}, bf16[1,1,32,2048]{3,2,1,0:T(8,128)(2,1)}, u32[]{:S(2)}) copy-start(bf16[1,1,32,2048]{3,2,1,0:T(8,128)(2,1)} %param.16) | copy-start | bytes 393220
  106.6 3.8 %collective-permute-start = (bf16[4,1024]{1,0:T(4,128)(2,1)S(1)}, bf16[4,1024]{1,0:T(4,128)(2,1)S(1)}, u32[]{:S(2)}, u32[]{:S(2)}) collective-permute-start(bf16[4,1024]{1,0:T(4,128)(2,1)S(1)} %reshape.98), channel_id=1, source_target_pairs={{2,0},{0,2},{3,1},{1,3},{6,4},{4,6},{7,5},{5,7},{10,8},{8,10},{11,... | collective-permute-start | bytes 24584 | tf_op jit(solution)/shard_map/ppermute | solution.py:27
  110.4 105.6 %collective-permute-start.1 = (bf16[4,1024]{1,0:T(4,128)(2,1)S(1)}, bf16[4,1024]{1,0:T(4,128)(2,1)S(1)}, u32[]{:S(2)}, u32[]{:S(2)}) collective-permute-start(bf16[4,1024]{1,0:T(4,128)(2,1)S(1)} %pad_select_fusion.1), channel_id=1, source_target_pairs={{2,0},{0,2},{3,1},{1,3},{6,4},{4,6},{7,5},{5,7},{10,8},{8,10},{11,... | collective-permute-start | bytes 24584 | tf_op jit(solution)/shard_map/ppermute | solution.py:27
  164.2 6.4 %slice-start = ((bf16[32,295040]{1,0:T(8,128)(2,1)}), bf16[32,294912]{1,0:T(8,128)(2,1)S(1)}, s32[]{:S(2)}) async-start(bf16[32,295040]{1,0:T(8,128)(2,1)} %tile.13), calls=%async_computation.1 | async-start | bytes 37748736 | tf_op jit(solution)/shard_map/slice | solution.py:72
  187.2 22.1 %copy-start.1 = (f32[4,2,257]{2,1,0:T(2,128)S(1)}, f32[4,2,257]{2,1,0:T(2,128)}, u32[]{:S(2)}) copy-start(f32[4,2,257]{2,1,0:T(2,128)} %param.19) | copy-start | bytes 24676
  213.2 1.4 slice-start.1
  228.8 9.0 %all-to-all-start = ((f32[1,2,2,4,1024]{4,2,1,0,3:T(2,128)}), f32[1,2,2,4,1024]{4,2,1,0,3:T(2,128)S(1)}, u32[]{:S(2)}, u32[]{:S(2)}) async-start(f32[1,2,2,4,1024]{4,2,1,0,3:T(2,128)} %copy.84), calls=%async_computation | async-start | bytes 131072 | tf_op jit(solution)/shard_map/all_to_all | solution.py:190
  237.8 6.5 %collective-permute-start.3 = (f32[4,2,2,128]{3,2,1,0:T(2,128)S(1)}, f32[4,2,2,128]{3,2,1,0:T(2,128)S(1)}, u32[]{:S(2)}, u32[]{:S(2)}) collective-permute-start(f32[4,2,2,128]{3,2,1,0:T(2,128)S(1)} %get-tuple-element.63), channel_id=1, source_target_pairs={{2,0},{4,2},{6,4},{8,6},{10,8},{12,10},{14,12},{3,1},{5,3},{7,5},{... | collective-permute-start | bytes 24584 | tf_op jit(solution)/shard_map/ppermute | solution.py:38
  239.1 5.9 %collective-permute-start.2 = (f32[4,2,2,128]{3,2,1,0:T(2,128)S(1)}, f32[4,2,2,128]{3,2,1,0:T(2,128)S(1)}, u32[]{:S(2)}, u32[]{:S(2)}) collective-permute-start(f32[4,2,2,128]{3,2,1,0:T(2,128)S(1)} %get-tuple-element.62), channel_id=1, source_target_pairs={{0,2},{2,4},{4,6},{6,8},{8,10},{10,12},{12,14},{1,3},{3,5},{5,7},{... | collective-permute-start | bytes 24584 | tf_op jit(solution)/shard_map/ppermute | solution.py:35
where the time goes:
time: 249 us; the launch traced here: 248 us
  local copies, waits for them, and re-layouts  107 us (43%)
  blocking collectives  70 us (28%)
  matrix products  49.3 us (20%)
  starting transfers between devices  11.3 us (5%)
  waiting for transfers between devices  6.3 us (3%)
    all_gather x2, blocking collectives, entering(): gathered = jax.tree.map(lambda a: lax.all_gather(a, axis), part)  54 us
    another operation x2, local copies, waits for them, and re-layouts, toeplitz_basis(): tiled = jnp.tile(spread, (1, frame_len))[:, :frame_len * line_len]  51.7 us
    unnamed x34, local copies, waits for them, and re-layouts  32 us
    all_gather x1, blocking collectives, body(): gathered = lax.all_gather(own_row, 'bank', axis=0, tiled=True)  11.9 us
    dot_general x1, matrix products, body(): jnp.dot(sin_table, imag_part * bin_scale, precision=HIGHEST)  10.4 us
    dot_general x1, matrix products, body(): jnp.dot(cos_table, real_part * bin_scale, precision=HIGHEST)  10.4 us
    dot_general x1, matrix products, toeplitz_basis(): jnp.einsum('brfm,imrq->bifq', stacked, table, preferred_element_type=jnp....  8.84 us
    dot_general x1, matrix products, body(): imag_part = jnp.dot(signal, sin_table, precision=HIGHEST)  8.79 us
  transfers between devices with their start and end apart: 5, of which 2 were waited for; matrix products, arithmetic and copies ran while one was open for 39% of the time, Pallas kernels for 0%

commit v1 on v0

v1 whole, which is shorter than its diff:
```python
import functools
import math

import jax
import jax.numpy as jnp
import numpy as np
from jax import lax
from jax.experimental import pallas as pl
from jax.experimental.pallas import tpu as pltpu
from jax.sharding import PartitionSpec as P

HIGHEST = lax.Precision.HIGHEST
LANES = 128
F32 = jnp.float32
BF16 = jnp.bfloat16


def swapped(block, axis, distance):
    route = [(i, i ^ distance) for i in range(lax.axis_size(axis))]
    return lax.ppermute(block, axis, route)


def tables(length):
    rows = length // LANES
    high = length // 2 // LANES
    lane = np.arange(LANES)
    turn = 2.0 * math.pi
    outer = turn * (np.arange(rows)[:, None] * lane[None, :] % rows) / rows
    outer = np.stack([np.cos(outer), np.sin(outer)])
    inner = turn * (lane[:, None] * lane[None, :]) / length
    inner = np.concatenate([np.cos(inner), np.sin(inner)], axis=1)
    shift = turn * (np.arange(high)[:, None] * lane[None, :] % rows) / rows
    shift = np.stack([np.cos(shift), np.sin(shift)])
    bins = np.arange(length // 2)
    full = turn * (bins[:, None] * lane[None, :] % length) / length
    full = np.concatenate([np.cos(full), np.sin(full)], axis=0)
    weight = np.where(bins == 0, 1.0 / length, 2.0 / length).reshape(high, LANES)
    return tuple(a.astype(np.float32) for a in (outer, inner, shift, full, weight))


def split_two(value):
    upper = value.astype(BF16)
    return upper, (value - upper.astype(F32)).astype(BF16)


def circulant(row):
    spread = jnp.broadcast_to(row, (LANES, LANES))
    return pltpu.roll(spread, 0, 1, stride=1, stride_axis=0)


def keep_right():
    u = lax.broadcasted_iota(jnp.int32, (LANES, LANES), 0)
    q = lax.broadcasted_iota(jnp.int32, (LANES, LANES), 1)
    return q >= u


def spectrum_kernel(strain, mask, reset, psd_ref, psd_rate, outer, inner, shift, out):
    rows = strain.shape[0]
    high = psd_ref.shape[0]
    signal = strain[...] * mask[...].astype(F32)
    left = []
    for part in range(2):
        for kh in range(high):
            left.append(signal * shift[part, kh : kh + 1, :])
    product = lax.dot_general(
        jnp.concatenate(left, axis=0),
        inner[...],
        (((1,), (0,)), ((), ())),
        precision=HIGHEST,
        preferred_element_type=F32,
    )
    cos_one, sin_one = outer[0], outer[1]
    real_rows, imag_rows = [], []
    for kh in range(high):
        with_cos = product[kh * rows : (kh + 1) * rows]
        with_sin = product[(high + kh) * rows : (high + kh + 1) * rows]
        cos_sum = with_cos[:, :LANES] - with_sin[:, LANES:]
        sin_sum = with_cos[:, LANES:] + with_sin[:, :LANES]
        real_rows.append(jnp.sum(cos_one * cos_sum - sin_one * sin_sum, axis=0, keepdims=True))
        imag_rows.append(jnp.sum(sin_one * cos_sum + cos_one * sin_sum, axis=0, keepdims=True))
    real_part = jnp.concatenate(real_rows, axis=0)
    imag_part = jnp.concatenate(imag_rows, axis=0)
    reference_psd = psd_ref[...]
    rate = psd_rate[...]
    power = (real_part * real_part + imag_part * imag_part) / (rows * LANES / 2)
    log_power = jnp.log(power + 0.1 * reference_psd)
    keep = (1.0 - rate) * (1.0 - 0.5 * reset[0].astype(F32))
    first = (lax.axis_index("bank") == 0) & (lax.axis_index("tm") == 0)
    drive = rate * log_power + jnp.where(first, keep * jnp.log(reference_psd), 0.0)
    whole = jnp.concatenate([real_part, imag_part, drive, keep], axis=0)
    upper, lower = split_two(whole)
    out[: 4 * high] = upper
    out[4 * high :] = lower


def filter_kernel(filters, mixing, count, out):
    total, basis = mixing.shape
    share = total // 2
    templ = share // 2
    rate = lax.axis_index("rate")
    row = lax.broadcasted_iota(jnp.int32, (total, total), 0)
    col = lax.broadcasted_iota(jnp.int32, (total, total), 1)
    part = (row // share) ^ rate
    source = (part * templ + row % templ) * 2 + row % share // templ
    choose = (col == source).astype(BF16)
    ordered = jnp.dot(choose, mixing[...], preferred_element_type=F32)
    live = lax.broadcasted_iota(jnp.int32, (total, basis), 1) < count[0]
    ordered = jnp.where(live, ordered, 0.0).astype(BF16)
    combined = jnp.dot(ordered, filters[...], preferred_element_type=F32)
    lags = filters.shape[1] // LANES
    low_half = lax.broadcasted_iota(jnp.int32, (total, LANES), 0) < share
    own, other = [], []
    for a in range(0, lags, 2):
        even = combined[:, a * LANES : (a + 1) * LANES]
        odd = combined[:, (a + 1) * LANES : (a + 2) * LANES]
        own.append(jnp.where(low_half, even, pltpu.roll(odd, share, 0)))
        other.append(jnp.where(low_half, pltpu.roll(even, share, 0), odd))
    out[...] = jnp.concatenate(own + other, axis=0).astype(BF16)


def band_kernel(series, upper_out, lower_out, lag_out):
    right = keep_right()
    for b in range(series.shape[0]):
        lag = jnp.zeros((1, 1), F32)
        for part in range(2):
            row = series[b, part : part + 1, :]
            lag = lag + jnp.sum(row * row, axis=1, keepdims=True)
            before = jnp.zeros((LANES, LANES), F32)
            for d in range(3):
                now = circulant(row[:, d * LANES : (d + 1) * LANES])
                upper, lower = split_two(jnp.where(right, now, before))
                upper_out[b, part * LANES : (part + 1) * LANES, d * LANES : (d + 1) * LANES] = upper
                lower_out[b, part * LANES : (part + 1) * LANES, d * LANES : (d + 1) * LANES] = lower
                before = now
        lag_out[b] = jnp.broadcast_to(lag, (8, LANES))


def output_kernel(
    own_a, own_b, other_a, other_b, full, outer, weight, band_up, band_low, lag,
    snr_out, chi_out, spec, logs, toeplitz, *, banks, tms, length, taps, window,
):
    rows = length // LANES
    high = length // 2 // LANES
    spec_rows = 8 * high
    lags = taps // LANES
    lag_rows = lags * 4
    piece_rows = tms * spec_rows + 2 * lag_rows
    pieces = banks * tms
    behind = -(-(taps + window) // length)
    near = behind + 2
    half = max(banks // 2, 1)
    bank = lax.axis_index("bank")
    tm = lax.axis_index("tm")
    place = bank * tms + tm
    bufs = ((own_a, own_b), (other_a, other_b))

    def piece(c, d):
        return bufs[c][d // half], (d % half) * piece_rows

    zero = jnp.zeros((4 * high, LANES), F32)
    for c in range(2):
        for i in range(behind):
            spec[c, i] = zero
            logs[c, i] = zero[:high]
        spec[c, pieces + behind] = zero
        logs[c, pieces + behind] = zero[:high]
        for d in range(banks):
            ref, start = piece(c, d)
            for e in range(tms):
                top = start + e * spec_rows
                value = ref[top : top + 4 * high].astype(F32)
                value = value + ref[top + 4 * high : top + 8 * high].astype(F32)
                spec[c, ((bank ^ d) * tms + (tm ^ e)) + behind] = value

    def advance(g, states):
        nexts = []
        for c in range(2):
            drive = spec[c, g + behind, 2 * high : 3 * high]
            keep = spec[c, g + behind, 3 * high : 4 * high]
            nexts.append(keep * states[c] + drive)
            logs[c, g + behind] = nexts[c]
        return tuple(nexts)

    states = (zero[:high], zero[:high])
    if pieces <= 16:
        for g in range(pieces):
            states = advance(g, states)
    else:
        lax.fori_loop(0, pieces, advance, states)

    cos_one, sin_one = outer[0], outer[1]
    left = []
    for c in range(2):
        for i in range(near):
            scale = jnp.exp(-0.5 * logs[c, place + i]) * weight[...]
            real = spec[c, place + i, :high] * scale
            imag = spec[c, place + i, high : 2 * high] * scale
            cos_parts, sin_parts = [], []
            for kh in range(high):
                re = jnp.broadcast_to(real[kh : kh + 1], (rows, LANES))
                im = jnp.broadcast_to(imag[kh : kh + 1], (rows, LANES))
                cos_parts.append(re * cos_one + im * sin_one)
                sin_parts.append(im * cos_one - re * sin_one)
            left.append(jnp.concatenate(cos_parts + sin_parts, axis=1))
    white = lax.dot_general(
        jnp.concatenate(left, axis=0),
        full[...],
        (((1,), (0,)), ((), ())),
        precision=HIGHEST,
        preferred_element_type=F32,
    )
    white = white.astype(BF16).astype(F32)

    first_out = behind * rows - 1
    out_frames = rows + 2
    first_t = first_out - (lags - 1)
    t_frames = lags - 1 + out_frames
    right = keep_right()
    for c in range(2):
        base = c * near * rows
        before = circulant(white[base + first_t - 1 : base + first_t])
        for s in range(t_frames):
            at = base + first_t + s
            now = circulant(white[at : at + 1])
            toeplitz[c * LANES : (c + 1) * LANES, s * LANES : (s + 1) * LANES] = jnp.where(
                right, now, before
            ).astype(BF16)
            before = now

    low_half = lax.broadcasted_iota(jnp.int32, (8, LANES), 0) < 4
    low_phase = lax.broadcasted_iota(jnp.int32, (8, LANES), 0) % 4 < 2
    after = jnp.where(place == pieces - 1, 0.0, 1.0).astype(F32)
    lane_row = lax.broadcasted_iota(jnp.int32, (LANES, LANES), 0)
    lane_col = lax.broadcasted_iota(jnp.int32, (LANES, LANES), 1)
    upto = (lane_row <= lane_col).astype(BF16)
    sums = jnp.concatenate([upto, jnp.ones((LANES, LANES), BF16)], axis=1)

    def conv(d):
        parts = []
        for c in range(2):
            ref, start = piece(c, d)
            top = start + tms * spec_rows + c * lag_rows
            parts.append(ref[top : top + lag_rows])
        return jnp.concatenate(parts, axis=1)

    def frames_of(g_all, row):
        accs = []
        for n in range(out_frames + 1):
            acc = None
            for a in range(lags // 2):
                s = n - 1 + (lags - 1) - 2 * a
                if 0 <= s < t_frames:
                    tile = g_all[row + 8 * a : row + 8 * a + 8, s * LANES : (s + 1) * LANES]
                    acc = tile if acc is None else acc + tile
            accs.append(acc)
        return [accs[n + 1] + pltpu.roll(accs[n], 4, 0) for n in range(out_frames)]

    for group in range(0, banks, 4):
        members = range(group, min(group + 4, banks))
        f_all = jnp.concatenate([conv(d) for d in members], axis=0)
        g_all = jnp.dot(f_all, toeplitz[...], preferred_element_type=F32)
        for first in range(0, len(members), 2):
            d0, d1 = members[first], members[first + 1]
            z0 = frames_of(g_all, first * lag_rows)
            z1 = frames_of(g_all, (first + 1) * lag_rows)
            z = [jnp.where(low_half, p, pltpu.roll(q, 4, 0)) for p, q in zip(z0, z1)]
            z[-1] = z[-1] * after
            stacked = jnp.concatenate(
                [jnp.concatenate(z[n : n + rows], axis=0) for n in range(3)], axis=1
            )
            up, low = split_two(stacked)
            corr = []
            for d in (d0, d1):
                b_up = band_up[bank ^ d]
                b_low = band_low[bank ^ d]
                dims = (((1,), (1,)), ((), ()))
                corr.append(
                    lax.dot_general(up, b_up, dims, preferred_element_type=F32)
                    + lax.dot_general(low, b_up, dims, preferred_element_type=F32)
                    + lax.dot_general(up, b_low, dims, preferred_element_type=F32)
                )
            power = []
            for v in z:
                square = v * v
                power.append(square + pltpu.roll(square, 6, 0))
            p_up, p_low = split_two(jnp.concatenate(power, axis=0))
            run = jnp.dot(p_up, sums, preferred_element_type=F32) + jnp.dot(
                p_low, sums, preferred_element_type=F32
            )
            lag_now = jnp.where(low_half, lag[bank ^ d0], lag[bank ^ d1])
            for n in range(rows):
                tile = slice(8 * n, 8 * n + 8)
                c_re = jnp.where(low_half, corr[0][tile, :LANES], corr[1][tile, :LANES])
                c_im = jnp.where(low_half, corr[0][tile, LANES:], corr[1][tile, LANES:])
                mid = z[n + 1]
                turned = jnp.where(low_phase, -pltpu.roll(mid, 6, 0), pltpu.roll(mid, 2, 0))
                cross = mid * c_re + turned * c_im
                cross = cross + pltpu.roll(cross, 6, 0)
                prev = slice(8 * n, 8 * n + 8)
                here = slice(8 * n + 8, 8 * n + 16)
                nxt = slice(8 * n + 16, 8 * n + 24)
                win = (run[prev, LANES:] - run[prev, :LANES] + power[n]) + (
                    run[here, LANES:] + run[nxt, :LANES]
                )
                energy = power[n + 1]
                chi = (win - 2.0 * cross + energy * lag_now) / (2 * window + 1)
                lanes = slice(n * LANES, (n + 1) * LANES)
                snr_out[bank ^ d0, :, lanes] = energy[0:2]
                snr_out[bank ^ d1, :, lanes] = energy[4:6]
                chi_out[bank ^ d0, :, lanes] = chi[0:2]
                chi_out[bank ^ d1, :, lanes] = chi[4:6]


VMEM = pl.BlockSpec(memory_space=pltpu.VMEM)
SMEM = pl.BlockSpec(memory_space=pltpu.SMEM)


def body(
    strain, gate_mask, psd_reset, psd_ref, psd_rate, filters, basis_count, mixing, autocorrelation
):
    length = strain.shape[1]
    rows = length // LANES
    high = length // 2 // LANES
    banks = lax.axis_size("bank")
    tms = lax.axis_size("tm")
    basis, taps = filters.shape[2:]
    templ = mixing.shape[2]
    window = autocorrelation.shape[2] // 2
    lags = taps // LANES
    outer, inner, shift, full, weight = tables(length)

    spec = pl.pallas_call(
        spectrum_kernel,
        out_shape=jax.ShapeDtypeStruct((8 * high, LANES), BF16),
        in_specs=[VMEM, VMEM, SMEM] + [VMEM] * 5,
        out_specs=VMEM,
        name="spectrum",
    )(
        strain.reshape(rows, LANES),
        gate_mask.reshape(rows, LANES),
        psd_reset,
        psd_ref.reshape(high, LANES),
        psd_rate.reshape(high, LANES),
        outer,
        inner,
        shift,
    )
    combined = pl.pallas_call(
        filter_kernel,
        out_shape=jax.ShapeDtypeStruct((2 * templ * lags, LANES), BF16),
        in_specs=[VMEM, VMEM, SMEM],
        out_specs=VMEM,
        name="filters",
    )(filters.reshape(basis, taps), mixing.reshape(2 * templ, basis), basis_count)
    padded = jnp.pad(autocorrelation, ((0, 0), (0, 0), (0, 3 * LANES - 2 * window - 1)))
    band = jax.ShapeDtypeStruct((banks, 2 * LANES, 3 * LANES), BF16)
    band_up, band_low, lag = pl.pallas_call(
        band_kernel,
        out_shape=(band, band, jax.ShapeDtypeStruct((banks, 8, LANES), F32)),
        in_specs=[VMEM],
        out_specs=(VMEM, VMEM, VMEM),
        name="bands",
    )(padded)

    distance = 1
    while distance < tms:
        spec = jnp.concatenate([spec, swapped(spec, "tm", distance)])
        distance *= 2
    held = jnp.concatenate([spec, combined])
    distance = 1
    while distance * 2 < banks:
        held = jnp.concatenate([held, swapped(held, "bank", distance)])
        distance *= 2
    far = swapped(held, "bank", distance)
    held_other = swapped(held, "rate", 1)
    far_other = swapped(far, "rate", 1)

    behind = -(-(taps + window) // length)
    near = behind + 2
    share = templ // 2
    out = jax.ShapeDtypeStruct((banks, share, length), F32)
    return pl.pallas_call(
        functools.partial(
            output_kernel, banks=banks, tms=tms, length=length, taps=taps, window=window
        ),
        out_shape=(out, out),
        in_specs=[VMEM] * 10,
        out_specs=(VMEM, VMEM),
        scratch_shapes=[
            pltpu.VMEM((2, banks * tms + behind + 1, 4 * high, LANES), F32),
            pltpu.VMEM((2, banks * tms + behind + 1, high, LANES), F32),
            pltpu.VMEM((2 * LANES, (lags + rows + 1) * LANES), BF16),
        ],
        name="outputs",
    )(held, far, held_other, far_other, full, outer, weight, band_up, band_low, lag)


def solution(mesh):
    return jax.shard_map(
        body,
        mesh=mesh,
        in_specs=(
            P("rate", ("parts", "bank", "tm")),
            P(("parts", "bank", "tm")),
            P(("parts", "bank", "tm")),
            P("rate", None),
            P("rate", None),
            P("bank", "rate", None, None),
            P("bank"),
            P("bank", "rate", None, None, None),
            P(),
        ),
        out_specs=(
            P(None, "rate", ("parts", "bank", "tm")),
            P(None, "rate", ("parts", "bank", "tm")),
        ),
        check_vma=False,
    )
```

time: 249 us -> 27.7 us (0.11)
  local copies, waits for them, and re-layouts: 107 us -> 1.28 us
  blocking collectives: 70 us -> 0 us
  matrix products: 49.3 us -> 0 us
  Pallas kernels: 0 us -> 10.5 us
  starting transfers between devices: 11.3 us -> 7.2 us
    all_gather x5 -> x0, blocking collectives: 70 us -> none  [the longest x2 54 us: entering(): gathered = jax.tree.map(lambda a: lax.all_gather(a, axis), part)]
    another operation x10 -> x0, local copies, waits for them, and re-layouts: 56.1 us -> none  [the longest x2 51.7 us: toeplitz_basis(): tiled = jnp.tile(spread, (1, frame_len))[:, :frame_len * line_len]]
    dot_general x8 -> x0, matrix products: 49.3 us -> none  [the longest x1 10.4 us: body(): jnp.dot(sin_table, imag_part * bin_scale, precision=HIGHEST)]
    unnamed x34 -> x14, local copies, waits for them, and re-layouts: 32 us -> 0.66 us
    slice x9 -> x0, local copies, waits for them, and re-layouts: 15.3 us -> none  [the longest x1 7.01 us: toeplitz_basis(): shifted[:, :, frame_len:frame_len + lag_count * frame_len]]
    pallas_call x0 -> x4, Pallas kernels: none -> 10.5 us  [the longest x1 4.48 us: body(): pl.pallas_call(functools.partial(output_kernel, banks=banks, tms=tms, len...]
    all_to_all x1 -> x0, waiting for transfers between devices: 5.59 us -> none  [body(): lax.all_to_all(snr_part[None], 'bank', split_axis=3, concat_axis=0, tiled...]
    ppermute x4 -> x5, waiting for transfers between devices: 0.7 us -> 5.46 us  [swapped(): return lax.ppermute(block, axis, route)]
  transfers between devices with their start and end apart: 5 -> 5, of which waited for: 2 -> 2; matrix products, arithmetic and copies ran while one was open for 39% -> 2% of each run, Pallas kernels for 0% -> 16%
where the time goes in v1:
time: 27.7 us; the launch traced here: 27.3 us
  Pallas kernels  10.5 us (38%)
  starting transfers between devices  7.2 us (26%)
  waiting for transfers between devices  5.46 us (20%)
  between operations  1.99 us (7%)
  local copies, waits for them, and re-layouts  1.28 us (5%)
  other arithmetic  0.83 us (3%)
    ppermute x5, starting transfers between devices, swapped(): return lax.ppermute(block, axis, route)  7.2 us
    ppermute x5, waiting for transfers between devices, swapped(): return lax.ppermute(block, axis, route)  5.46 us
    pallas_call x1, Pallas kernels, body(): pl.pallas_call(functools.partial(output_kernel, banks=banks, tms=tms, len...  4.48 us
    pallas_call x1, Pallas kernels, body(): pl.pallas_call(band_kernel, out_shape=(band, band, jax.ShapeDtypeStruct((...  2.45 us
    pallas_call x1, Pallas kernels, body(): pl.pallas_call(filter_kernel, out_shape=jax.ShapeDtypeStruct((2 * templ *...  1.8 us
    pallas_call x1, Pallas kernels, body(): pl.pallas_call(spectrum_kernel, out_shape=jax.ShapeDtypeStruct((8 * high,...  1.78 us
    concatenate x1, other arithmetic, body(): held = jnp.concatenate([spec, combined])  0.82 us
    unnamed x14, local copies, waits for them, and re-layouts  0.66 us
  transfers between devices with their start and end apart: 5, of which 2 were waited for; matrix products, arithmetic and copies ran while one was open for 2% of the time, Pallas kernels for 16%

profile of v1, /device:TPU:0, one launch (start us, length us, event | category | flops | bytes accessed | tf_op | source)
XLA Modules:
  0.0 27.3 jit_solution(5258248116509359241)
XLA Ops:
  1.3 1.8 %spectrum.1 = bf16[32,128]{1,0:T(8,128)(2,1)} custom-call(f32[8,128]{1,0:T(8,128)} %bitcast.7, s32[8,128]{1,0:T(8,128)} %bitcast.8, s32[1]{0:T(128)S(6)} %copy.16.reset, f32[4,128]{1,0:T(4,128)} %bitcast.9, f32[4,128]{1,0:T(4,128)} %bitcast.10, f32[2,8,128]{2,1,0:T(8,128)} %constant.13.clone.outer, f32[128,256]{1,0:T(8,128)} %constant.14.clone.inner, ...), custom_call_target="tpu_custom_call" | custom-call | tf_op jit(solution)/shard_map/spectrum/pallas_call | solution.py:332
  3.1 3.0 %collective-permute-start = (bf16[32,128]{1,0:T(8,128)(2,1)}, bf16[32,128]{1,0:T(8,128)(2,1)S(1)}, u32[]{:S(2)}, u32[]{:S(2)}) collective-permute-start(bf16[32,128]{1,0:T(8,128)(2,1)} %spectrum.1), channel_id=1, source_target_pairs={{0,2},{2,0},{1,3},{3,1},{4,6},{6,4},{5,7},{7,5},{8,10},{10,8},{9,1... | collective-permute-start | bytes 24584 | tf_op jit(solution)/shard_map/ppermute | solution.py:20
  6.7 0.0 copy-start.5
  6.7 1.8 %filters.1 = bf16[128,128]{1,0:T(8,128)(2,1)} custom-call(bf16[32,2048]{1,0:T(8,128)(2,1)} %bitcast.6, bf16[8,32]{1,0:T(8,128)(2,1)} %bitcast.11, s32[1]{0:T(128)S(6)} %copy.17.count), custom_call_target="tpu_custom_call" | custom-call | tf_op jit(solution)/shard_map/filters/pallas_call | solution.py:348
  8.5 0.0 copy-start.1
  8.5 0.0 collective-permute-done
  8.5 0.0 copy-done.5
  8.5 0.8 %pad_maximum_fusion.1 = bf16[192,128]{1,0:T(8,128)(2,1)S(1)} fusion(bf16[128,128]{1,0:T(8,128)(2,1)} %filters.1, bf16[32,128]{1,0:T(8,128)(2,1)S(1)} %collective-permute-done, bf16[32,128]{1,0:T(8,128)(2,1)S(1)} %copy-done.5), kind=kLoop, calls=%fused_computation.1 | loop fusion | flops 147456 | bytes 98304 | tf_op jit(solution)/shard_map/concatenate | solution.py:369
  9.3 0.0 copy-start.6
  9.3 1.6 %collective-permute-start.1 = (bf16[192,128]{1,0:T(8,128)(2,1)S(1)}, bf16[192,128]{1,0:T(8,128)(2,1)S(1)}, u32[]{:S(2)}, u32[]{:S(2)}) collective-permute-start(bf16[192,128]{1,0:T(8,128)(2,1)S(1)} %pad_maximum_fusion.1), channel_id=1, source_target_pairs={{0,4},{4,0},{8,12},{12,8},{1,5},{5,1},{9,13},{13,9},{2,6},{6,2},{1... | collective-permute-start | bytes 147464 | tf_op jit(solution)/shard_map/ppermute | solution.py:20
  10.9 2.5 %collective-permute-done.1 = bf16[192,128]{1,0:T(8,128)(2,1)S(1)} collective-permute-done((bf16[192,128]{1,0:T(8,128)(2,1)S(1)}, bf16[192,128]{1,0:T(8,128)(2,1)S(1)}, u32[]{:S(2)}, u32[]{:S(2)}) %collective-permute-start.1) | collective-permute-done | bytes 49184 | tf_op jit(solution)/shard_map/ppermute | solution.py:20
  13.4 0.0 copy-done.1
  13.4 0.0 copy-start
  13.4 2.7 %collective-permute-start.2 = (bf16[384,128]{1,0:T(8,128)(2,1)S(1)}, bf16[384,128]{1,0:T(8,128)(2,1)S(1)}, u32[]{:S(2)}, u32[]{:S(2)}) collective-permute-start(bf16[384,128]{1,0:T(8,128)(2,1)S(1)} %pad_maximum_fusion.own_a), channel_id=1, source_target_pairs={{0,8},{4,12},{8,0},{12,4},{1,9},{5,13},{9,1},{13,5},{2,10},{6,14},... | collective-permute-start | bytes 294920 | tf_op jit(solution)/shard_map/ppermute | solution.py:20
  16.1 0.0 collective-permute-start.3
  16.1 2.9 %collective-permute-done.2.own_b = bf16[384,128]{1,0:T(8,128)(2,1)S(1)} collective-permute-done((bf16[384,128]{1,0:T(8,128)(2,1)S(1)}, bf16[384,128]{1,0:T(8,128)(2,1)S(1)}, u32[]{:S(2)}, u32[]{:S(2)}) %collective-permute-start.2) | collective-permute-done | bytes 98336 | tf_op jit(solution)/shard_map/ppermute | solution.py:20
  19.0 0.0 copy-start.2
  19.0 0.0 collective-permute-start.4
  19.0 0.0 copy-done.6
  19.0 0.6 %pad.4.series = f32[4,2,384]{2,1,0:T(2,128)} pad(f32[4,2,257]{2,1,0:T(2,128)S(1)} %copy-done.6, f32[]{:T(128)} %constant.12.clone.1), padding=0_0x0_0x0_127 | pad | bytes 20516 | tf_op jit(solution)/shard_map/jit(_pad)/pad | solution.py:355
  19.7 2.4 %bands.1 = (bf16[4,256,384]{2,1,0:T(8,128)(2,1)}, bf16[4,256,384]{2,1,0:T(8,128)(2,1)}, f32[4,8,128]{2,1,0:T(8,128)}) custom-call(f32[4,2,384]{2,1,0:T(2,128)} %pad.4.series), custom_call_target="tpu_custom_call" | custom-call | tf_op jit(solution)/shard_map/bands/pallas_call | solution.py:357
  22.1 0.0 collective-permute-done.3.other_a
  22.1 0.0 copy-start.3
  22.1 0.0 collective-permute-done.4.other_b
  22.1 0.0 copy-start.4
  22.1 0.0 copy-done
  22.1 0.0 copy-done.2
  22.1 0.6 %copy-done.3 = bf16[384,128]{1,0:T(8,128)(2,1)} copy-done((bf16[384,128]{1,0:T(8,128)(2,1)}, bf16[384,128]{1,0:T(8,128)(2,1)S(1)}, u32[]{:S(2)}) %copy-start.3) | copy-done | bytes 98328
  22.8 0.0 copy-done.4
  22.8 4.5 %outputs.1 = (f32[4,2,1024]{2,1,0:T(2,128)}, f32[4,2,1024]{2,1,0:T(2,128)}) custom-call(bf16[384,128]{1,0:T(8,128)(2,1)} %copy-done, bf16[384,128]{1,0:T(8,128)(2,1)} %copy-done.2, bf16[384,128]{1,0:T(8,128)(2,1)} %copy-done.3, bf16[384,128]{1,0:T(8,128)(2,1)} %copy-done.4, f32[1024,128]{1,0:T(8,128)} %constant.16.clone.full, ...), custom_call_target="tpu_custom_call" | custom-call | tf_op jit(solution)/shard_map/outputs/pallas_call | solution.py:382
  (1 shorter events, 0.0 us)
Async XLA Ops:
  3.1 5.4 %collective-permute-start = (bf16[32,128]{1,0:T(8,128)(2,1)}, bf16[32,128]{1,0:T(8,128)(2,1)S(1)}, u32[]{:S(2)}, u32[]{:S(2)}) collective-permute-start(bf16[32,128]{1,0:T(8,128)(2,1)} %spectrum.1), channel_id=1, source_target_pairs={{0,2},{2,0},{1,3},{3,1},{4,6},{6,4},{5,7},{7,5},{8,10},{10,8},{9,1... | collective-permute-start | bytes 24584 | tf_op jit(solution)/shard_map/ppermute | solution.py:20
  6.7 1.8 %copy-start.5 = (bf16[32,128]{1,0:T(8,128)(2,1)S(1)}, bf16[32,128]{1,0:T(8,128)(2,1)}, u32[]{:S(2)}) copy-start(bf16[32,128]{1,0:T(8,128)(2,1)} %spectrum.1) | copy-start | bytes 24580
  8.5 4.9 %copy-start.1 = (bf16[128,128]{1,0:T(8,128)(2,1)S(1)}, bf16[128,128]{1,0:T(8,128)(2,1)}, u32[]{:S(2)}) copy-start(bf16[128,128]{1,0:T(8,128)(2,1)} %filters.1) | copy-start | bytes 98308
  9.3 9.7 %copy-start.6 = (f32[4,2,257]{2,1,0:T(2,128)S(1)}, f32[4,2,257]{2,1,0:T(2,128)}, u32[]{:S(2)}) copy-start(f32[4,2,257]{2,1,0:T(2,128)} %param.22) | copy-start | bytes 24676
  9.3 4.1 %collective-permute-start.1 = (bf16[192,128]{1,0:T(8,128)(2,1)S(1)}, bf16[192,128]{1,0:T(8,128)(2,1)S(1)}, u32[]{:S(2)}, u32[]{:S(2)}) collective-permute-start(bf16[192,128]{1,0:T(8,128)(2,1)S(1)} %pad_maximum_fusion.1), channel_id=1, source_target_pairs={{0,4},{4,0},{8,12},{12,8},{1,5},{5,1},{9,13},{13,9},{2,6},{6,2},{1... | collective-permute-start | bytes 147464 | tf_op jit(solution)/shard_map/ppermute | solution.py:20
  13.4 8.7 %copy-start = (bf16[384,128]{1,0:T(8,128)(2,1)}, bf16[384,128]{1,0:T(8,128)(2,1)S(1)}, u32[]{:S(2)}) copy-start(bf16[384,128]{1,0:T(8,128)(2,1)S(1)} %pad_maximum_fusion.own_a) | copy-start | bytes 294916
  13.4 5.6 %collective-permute-start.2 = (bf16[384,128]{1,0:T(8,128)(2,1)S(1)}, bf16[384,128]{1,0:T(8,128)(2,1)S(1)}, u32[]{:S(2)}, u32[]{:S(2)}) collective-permute-start(bf16[384,128]{1,0:T(8,128)(2,1)S(1)} %pad_maximum_fusion.own_a), channel_id=1, source_target_pairs={{0,8},{4,12},{8,0},{12,4},{1,9},{5,13},{9,1},{13,5},{2,10},{6,14},... | collective-permute-start | bytes 294920 | tf_op jit(solution)/shard_map/ppermute | solution.py:20
  16.1 6.0 %collective-permute-start.3 = (bf16[384,128]{1,0:T(8,128)(2,1)S(1)}, bf16[384,128]{1,0:T(8,128)(2,1)S(1)}, u32[]{:S(2)}, u32[]{:S(2)}) collective-permute-start(bf16[384,128]{1,0:T(8,128)(2,1)S(1)} %pad_maximum_fusion.own_a), channel_id=1, source_target_pairs={{0,1},{1,0},{2,3},{3,2},{4,5},{5,4},{6,7},{7,6},{8,9},{9,8},{10,11... | collective-permute-start | bytes 294920 | tf_op jit(solution)/shard_map/ppermute | solution.py:20
  19.0 3.1 %copy-start.2 = (bf16[384,128]{1,0:T(8,128)(2,1)}, bf16[384,128]{1,0:T(8,128)(2,1)S(1)}, u32[]{:S(2)}) copy-start(bf16[384,128]{1,0:T(8,128)(2,1)S(1)} %collective-permute-done.2.own_b) | copy-start | bytes 294916
  19.0 3.1 %collective-permute-start.4 = (bf16[384,128]{1,0:T(8,128)(2,1)S(1)}, bf16[384,128]{1,0:T(8,128)(2,1)S(1)}, u32[]{:S(2)}, u32[]{:S(2)}) collective-permute-start(bf16[384,128]{1,0:T(8,128)(2,1)S(1)} %collective-permute-done.2.own_b), channel_id=1, source_target_pairs={{0,1},{1,0},{2,3},{3,2},{4,5},{5,4},{6,7},{7,6},{8,9},{9,8},{10,11... | collective-permute-start | bytes 294920 | tf_op jit(solution)/shard_map/ppermute | solution.py:20
  22.1 0.7 %copy-start.3 = (bf16[384,128]{1,0:T(8,128)(2,1)}, bf16[384,128]{1,0:T(8,128)(2,1)S(1)}, u32[]{:S(2)}) copy-start(bf16[384,128]{1,0:T(8,128)(2,1)S(1)} %collective-permute-done.3.other_a) | copy-start | bytes 294916
  22.1 0.7 %copy-start.4 = (bf16[384,128]{1,0:T(8,128)(2,1)}, bf16[384,128]{1,0:T(8,128)(2,1)S(1)}, u32[]{:S(2)}) copy-start(bf16[384,128]{1,0:T(8,128)(2,1)S(1)} %collective-permute-done.4.other_b) | copy-start | bytes 294916

commit v2 on v1

--- a/solution.py
+++ b/solution.py
@@ -8,6 +8,7 @@
 from jax.experimental import pallas as pl
 from jax.experimental.pallas import tpu as pltpu
 from jax.sharding import PartitionSpec as P
+
 
 HIGHEST = lax.Precision.HIGHEST
 LANES = 128
@@ -34,8 +35,7 @@
     bins = np.arange(length // 2)
     full = turn * (bins[:, None] * lane[None, :] % length) / length
     full = np.concatenate([np.cos(full), np.sin(full)], axis=0)
-    weight = np.where(bins == 0, 1.0 / length, 2.0 / length).reshape(high, LANES)
-    return tuple(a.astype(np.float32) for a in (outer, inner, shift, full, weight))
+    return tuple(a.astype(np.float32) for a in (outer, inner, shift, full))
 
 
 def split_two(value):
@@ -124,6 +124,8 @@
         lag = jnp.zeros((1, 1), F32)
         for part in range(2):
             row = series[b, part : part + 1, :]
+            fill = jnp.zeros((1, 3 * LANES - row.shape[1]), F32)
+            row = jnp.concatenate([row, fill], axis=1)
             lag = lag + jnp.sum(row * row, axis=1, keepdims=True)
             before = jnp.zeros((LANES, LANES), F32)
             for d in range(3):
@@ -136,8 +138,8 @@
 
 
 def output_kernel(
-    own_a, own_b, other_a, other_b, full, outer, weight, band_up, band_low, lag,
-    snr_out, chi_out, spec, logs, toeplitz, *, banks, tms, length, taps, window,
+    own_a, own_b, other_a, other_b, full, outer, band_up, band_low, lag,
+    snr_out, chi_out, spec, logs, toeplitz, *, order, tms, length, taps, window,
 ):
     rows = length // LANES
     high = length // 2 // LANES
@@ -145,10 +147,11 @@
     lags = taps // LANES
     lag_rows = lags * 4
     piece_rows = tms * spec_rows + 2 * lag_rows
-    pieces = banks * tms
+    pieces = len(order) * tms
     behind = -(-(taps + window) // length)
     near = behind + 2
-    half = max(banks // 2, 1)
+    banks = len(order)
+    half = banks // 2
     bank = lax.axis_index("bank")
     tm = lax.axis_index("tm")
     place = bank * tms + tm
@@ -170,7 +173,7 @@
                 top = start + e * spec_rows
                 value = ref[top : top + 4 * high].astype(F32)
                 value = value + ref[top + 4 * high : top + 8 * high].astype(F32)
-                spec[c, ((bank ^ d) * tms + (tm ^ e)) + behind] = value
+                spec[c, ((bank ^ order[d]) * tms + (tm ^ e)) + behind] = value
 
     def advance(g, states):
         nexts = []
@@ -189,10 +192,13 @@
         lax.fori_loop(0, pieces, advance, states)
 
     cos_one, sin_one = outer[0], outer[1]
+    bin_row = lax.broadcasted_iota(jnp.int32, (high, LANES), 0)
+    bin_lane = lax.broadcasted_iota(jnp.int32, (high, LANES), 1)
+    weight = jnp.where(bin_row + bin_lane == 0, 1.0 / length, 2.0 / length).astype(F32)
     left = []
     for c in range(2):
         for i in range(near):
-            scale = jnp.exp(-0.5 * logs[c, place + i]) * weight[...]
+            scale = jnp.exp(-0.5 * logs[c, place + i]) * weight
             real = spec[c, place + i, :high] * scale
             imag = spec[c, place + i, high : 2 * high] * scale
             cos_parts, sin_parts = [], []
@@ -261,6 +267,7 @@
         g_all = jnp.dot(f_all, toeplitz[...], preferred_element_type=F32)
         for first in range(0, len(members), 2):
             d0, d1 = members[first], members[first + 1]
+            bank0, bank1 = bank ^ order[d0], bank ^ order[d1]
             z0 = frames_of(g_all, first * lag_rows)
             z1 = frames_of(g_all, (first + 1) * lag_rows)
             z = [jnp.where(low_half, p, pltpu.roll(q, 4, 0)) for p, q in zip(z0, z1)]
@@ -271,8 +278,8 @@
             up, low = split_two(stacked)
             corr = []
             for d in (d0, d1):
-                b_up = band_up[bank ^ d]
-                b_low = band_low[bank ^ d]
+                b_up = band_up[bank ^ order[d]]
+                b_low = band_low[bank ^ order[d]]
                 dims = (((1,), (1,)), ((), ()))
                 corr.append(
                     lax.dot_general(up, b_up, dims, preferred_element_type=F32)
@@ -287,7 +294,7 @@
             run = jnp.dot(p_up, sums, preferred_element_type=F32) + jnp.dot(
                 p_low, sums, preferred_element_type=F32
             )
-            lag_now = jnp.where(low_half, lag[bank ^ d0], lag[bank ^ d1])
+            lag_now = jnp.where(low_half, lag[bank0], lag[bank1])
             for n in range(rows):
                 tile = slice(8 * n, 8 * n + 8)
                 c_re = jnp.where(low_half, corr[0][tile, :LANES], corr[1][tile, :LANES])
@@ -305,10 +312,25 @@
                 energy = power[n + 1]
                 chi = (win - 2.0 * cross + energy * lag_now) / (2 * window + 1)
                 lanes = slice(n * LANES, (n + 1) * LANES)
-                snr_out[bank ^ d0, :, lanes] = energy[0:2]
-                snr_out[bank ^ d1, :, lanes] = energy[4:6]
-                chi_out[bank ^ d0, :, lanes] = chi[0:2]
-                chi_out[bank ^ d1, :, lanes] = chi[4:6]
+                snr_out[bank0, :, lanes] = energy[0:2]
+                snr_out[bank1, :, lanes] = energy[4:6]
+                chi_out[bank0, :, lanes] = chi[0:2]
+                chi_out[bank1, :, lanes] = chi[4:6]
+
+
+ON_CHIP_BYTES = 3 * 2**20
+
+
+def on_chip(*arrays):
+    if sum(a.size * a.dtype.itemsize for a in arrays) > ON_CHIP_BYTES:
+        return arrays
+    return [pltpu.with_memory_space_constraint(a, pltpu.VMEM) for a in arrays]
+
+
+def on_chip_shape(shape, dtype):
+    if 2 * math.prod(shape) * jnp.dtype(dtype).itemsize > ON_CHIP_BYTES:
+        return jax.ShapeDtypeStruct(shape, dtype)
+    return pltpu.VMEM(shape, dtype)
 
 
 VMEM = pl.BlockSpec(memory_space=pltpu.VMEM)
@@ -327,11 +349,11 @@
     templ = mixing.shape[2]
     window = autocorrelation.shape[2] // 2
     lags = taps // LANES
-    outer, inner, shift, full, weight = tables(length)
+    outer, inner, shift, full = tables(length)
 
     spec = pl.pallas_call(
         spectrum_kernel,
-        out_shape=jax.ShapeDtypeStruct((8 * high, LANES), BF16),
+        out_shape=pltpu.VMEM((8 * high, LANES), BF16),
         in_specs=[VMEM, VMEM, SMEM] + [VMEM] * 5,
         out_specs=VMEM,
         name="spectrum",
@@ -347,44 +369,45 @@
     )
     combined = pl.pallas_call(
         filter_kernel,
-        out_shape=jax.ShapeDtypeStruct((2 * templ * lags, LANES), BF16),
+        out_shape=pltpu.VMEM((2 * templ * lags, LANES), BF16),
         in_specs=[VMEM, VMEM, SMEM],
         out_specs=VMEM,
         name="filters",
     )(filters.reshape(basis, taps), mixing.reshape(2 * templ, basis), basis_count)
-    padded = jnp.pad(autocorrelation, ((0, 0), (0, 0), (0, 3 * LANES - 2 * window - 1)))
-    band = jax.ShapeDtypeStruct((banks, 2 * LANES, 3 * LANES), BF16)
+    band = on_chip_shape((banks, 2 * LANES, 3 * LANES), BF16)
     band_up, band_low, lag = pl.pallas_call(
         band_kernel,
-        out_shape=(band, band, jax.ShapeDtypeStruct((banks, 8, LANES), F32)),
+        out_shape=(band, band, pltpu.VMEM((banks, 8, LANES), F32)),
         in_specs=[VMEM],
         out_specs=(VMEM, VMEM, VMEM),
         name="bands",
-    )(padded)
+    )(autocorrelation)
 
     distance = 1
     while distance < tms:
         spec = jnp.concatenate([spec, swapped(spec, "tm", distance)])
         distance *= 2
     held = jnp.concatenate([spec, combined])
-    distance = 1
-    while distance * 2 < banks:
+    distance = banks // 2
+    order = [0]
+    while distance > 1:
         held = jnp.concatenate([held, swapped(held, "bank", distance)])
-        distance *= 2
-    far = swapped(held, "bank", distance)
+        order = order + [d ^ distance for d in order]
+        distance //= 2
+    far = swapped(held, "bank", 1)
+    order = order + [d ^ 1 for d in order]
     held_other = swapped(held, "rate", 1)
     far_other = swapped(far, "rate", 1)
 
     behind = -(-(taps + window) // length)
-    near = behind + 2
     share = templ // 2
     out = jax.ShapeDtypeStruct((banks, share, length), F32)
     return pl.pallas_call(
         functools.partial(
-            output_kernel, banks=banks, tms=tms, length=length, taps=taps, window=window
+            output_kernel, order=tuple(order), tms=tms, length=length, taps=taps, window=window
         ),
         out_shape=(out, out),
-        in_specs=[VMEM] * 10,
+        in_specs=[VMEM] * 9,
         out_specs=(VMEM, VMEM),
         scratch_shapes=[
             pltpu.VMEM((2, banks * tms + behind + 1, 4 * high, LANES), F32),
@@ -392,7 +415,7 @@
             pltpu.VMEM((2 * LANES, (lags + rows + 1) * LANES), BF16),
         ],
         name="outputs",
-    )(held, far, held_other, far_other, full, outer, weight, band_up, band_low, lag)
+    )(*on_chip(held, far, held_other, far_other, full, outer, band_up, band_low, lag))
 
 
 def solution(mesh):

time: 27.7 us -> 21.6 us (0.78)
  Pallas kernels: 10.5 us -> 6.4 us
  local copies, waits for them, and re-layouts: 1.28 us -> 0.01 us
  other arithmetic: 0.83 us -> 0.01 us
  starting transfers between devices: 7.2 us -> 7.71 us
    pallas_call x4, Pallas kernels: 10.5 us -> 6.4 us  [the longest x1 2.78 us: body(): pl.pallas_call(functools.partial(output_kernel, order=tuple(order), tms=t...]
    concatenate x1, other arithmetic: 0.82 us -> 0.01 us  [body(): held = jnp.concatenate([spec, combined])]
    unnamed x14 -> x4, local copies, waits for them, and re-layouts: 0.66 us -> 0.01 us
    pad x1 -> x0, local copies, waits for them, and re-layouts: 0.62 us -> none  [body(): jnp.pad(autocorrelation, ((0, 0), (0, 0), (0, 3 * LANES - 2 * window - 1)))]
    ppermute x5, starting transfers between devices: 7.2 us -> 7.71 us  [swapped(): return lax.ppermute(block, axis, route)]
  transfers between devices with their start and end apart: 5 -> 5, of which waited for: 2 -> 2; matrix products, arithmetic and copies ran while one was open for 2% -> 0% of each run, Pallas kernels for 16% -> 11%
where the time goes in v2:
time: 21.6 us; the launch traced here: 21.4 us
  starting transfers between devices  7.71 us (36%)
  Pallas kernels  6.4 us (30%)
  waiting for transfers between devices  5.19 us (24%)
  between operations  2.07 us (10%)
    ppermute x5, starting transfers between devices, swapped(): return lax.ppermute(block, axis, route)  7.71 us
    ppermute x5, waiting for transfers between devices, swapped(): return lax.ppermute(block, axis, route)  5.19 us
    pallas_call x1, Pallas kernels, body(): pl.pallas_call(functools.partial(output_kernel, order=tuple(order), tms=t...  2.78 us
    pallas_call x1, Pallas kernels, body(): pl.pallas_call(band_kernel, out_shape=(band, band, pltpu.VMEM((banks, 8,...  1.28 us
    pallas_call x1, Pallas kernels, body(): pl.pallas_call(filter_kernel, out_shape=pltpu.VMEM((2 * templ * lags, LAN...  1.17 us
    pallas_call x1, Pallas kernels, body(): pl.pallas_call(spectrum_kernel, out_shape=pltpu.VMEM((8 * high, LANES), B...  1.17 us
  transfers between devices with their start and end apart: 5, of which 2 were waited for; matrix products, arithmetic and copies ran while one was open for 0% of the time, Pallas kernels for 11%

profile of v2, /device:TPU:0, one launch (start us, length us, event | category | flops | bytes accessed | tf_op | source)
XLA Modules:
  0.0 21.4 jit_solution(3426798391499448829)
XLA Ops:
  0.6 0.0 copy-start
  1.3 1.2 %spectrum.1 = bf16[32,128]{1,0:T(8,128)(2,1)S(1)} custom-call(f32[8,128]{1,0:T(8,128)} %bitcast.7, s32[8,128]{1,0:T(8,128)} %bitcast.8, s32[1]{0:T(128)S(6)} %copy.15.reset, f32[4,128]{1,0:T(4,128)} %bitcast.9, f32[4,128]{1,0:T(4,128)} %bitcast.10, f32[2,8,128]{2,1,0:T(8,128)} %constant.8.clone.outer, f32[128,256]{1,0:T(8,128)} %constant.9.clone.inner, ...), custom_call_target="tpu_custom_call" | custom-call | tf_op jit(solution)/shard_map/spectrum/pallas_call | solution.py:354
  2.5 3.0 %collective-permute-start = (bf16[32,128]{1,0:T(8,128)(2,1)S(1)}, bf16[32,128]{1,0:T(8,128)(2,1)S(1)}, u32[]{:S(2)}, u32[]{:S(2)}) collective-permute-start(bf16[32,128]{1,0:T(8,128)(2,1)S(1)} %spectrum.1), channel_id=1, source_target_pairs={{0,2},{2,0},{1,3},{3,1},{4,6},{6,4},{5,7},{7,5},{8,10},{10,8},{9,1... | collective-permute-start | bytes 24584 | tf_op jit(solution)/shard_map/ppermute | solution.py:21
  6.2 1.2 %filters.1 = bf16[128,128]{1,0:T(8,128)(2,1)S(1)} custom-call(bf16[32,2048]{1,0:T(8,128)(2,1)} %bitcast.6, bf16[8,32]{1,0:T(8,128)(2,1)} %bitcast.11, s32[1]{0:T(128)S(6)} %copy.16.count), custom_call_target="tpu_custom_call" | custom-call | tf_op jit(solution)/shard_map/filters/pallas_call | solution.py:370
  7.4 0.0 collective-permute-done
  7.4 2.9 %collective-permute-start.1 = (bf16[192,128]{1,0:T(8,128)(2,1)S(1)}, bf16[192,128]{1,0:T(8,128)(2,1)S(1)}, u32[]{:S(2)}, u32[]{:S(2)}) collective-permute-start(bf16[192,128]{1,0:T(8,128)(2,1)S(1)} %pad_maximum_fusion.1), channel_id=1, source_target_pairs={{0,8},{4,12},{8,0},{12,4},{1,9},{5,13},{9,1},{13,5},{2,10},{6,14},... | collective-permute-start | bytes 147464 | tf_op jit(solution)/shard_map/ppermute | solution.py:21
  10.3 2.3 %collective-permute-done.1 = bf16[192,128]{1,0:T(8,128)(2,1)S(1)} collective-permute-done((bf16[192,128]{1,0:T(8,128)(2,1)S(1)}, bf16[192,128]{1,0:T(8,128)(2,1)S(1)}, u32[]{:S(2)}, u32[]{:S(2)}) %collective-permute-start.1) | collective-permute-done | bytes 49184 | tf_op jit(solution)/shard_map/ppermute | solution.py:21
  12.6 0.0 copy-start.1
  12.6 1.8 %collective-permute-start.2 = (bf16[384,128]{1,0:T(8,128)(2,1)S(1)}, bf16[384,128]{1,0:T(8,128)(2,1)S(1)}, u32[]{:S(2)}, u32[]{:S(2)}) collective-permute-start(bf16[384,128]{1,0:T(8,128)(2,1)S(1)} %pad_maximum_fusion.own_a), channel_id=1, source_target_pairs={{0,4},{4,0},{8,12},{12,8},{1,5},{5,1},{9,13},{13,9},{2,6},{6,2},{1... | collective-permute-start | bytes 294920 | tf_op jit(solution)/shard_map/ppermute | solution.py:21
  14.4 0.0 collective-permute-start.3
  14.4 2.9 %collective-permute-done.2.own_b = bf16[384,128]{1,0:T(8,128)(2,1)S(1)} collective-permute-done((bf16[384,128]{1,0:T(8,128)(2,1)S(1)}, bf16[384,128]{1,0:T(8,128)(2,1)S(1)}, u32[]{:S(2)}, u32[]{:S(2)}) %collective-permute-start.2) | collective-permute-done | bytes 98336 | tf_op jit(solution)/shard_map/ppermute | solution.py:21
  17.3 0.0 collective-permute-start.4
  17.3 1.3 %bands.1 = (bf16[4,256,384]{2,1,0:T(8,128)(2,1)S(1)}, bf16[4,256,384]{2,1,0:T(8,128)(2,1)S(1)}, f32[4,8,128]{2,1,0:T(8,128)S(1)}) custom-call(f32[4,2,257]{2,1,0:T(2,128)} %series.1), custom_call_target="tpu_custom_call" | custom-call | tf_op jit(solution)/shard_map/bands/pallas_call | solution.py:378
  18.6 0.0 collective-permute-done.3.other_a
  18.6 0.0 collective-permute-done.4.other_b
  18.6 0.0 copy-done
  18.6 0.0 copy-done.1
  18.6 2.8 %outputs.1 = (f32[4,2,1024]{2,1,0:T(2,128)}, f32[4,2,1024]{2,1,0:T(2,128)}) custom-call(bf16[384,128]{1,0:T(8,128)(2,1)S(1)} %pad_maximum_fusion.own_a, bf16[384,128]{1,0:T(8,128)(2,1)S(1)} %collective-permute-done.2.own_b, bf16[384,128]{1,0:T(8,128)(2,1)S(1)} %collective-permute-done.3.other_a, bf16[384,128]{1,0:T(8,128)(2,1)S(1)} %collective-permute-done.4.other_b, ...), custom_call_target="tpu_custom_call" | custom-call | tf_op jit(solution)/shard_map/outputs/pallas_call | solution.py:405
  (2 shorter events, 0.0 us)
Async XLA Ops:
  0.6 18.0 %copy-start = (f32[1024,128]{1,0:T(8,128)S(1)}, f32[1024,128]{1,0:T(8,128)}, u32[]{:S(2)}) copy-start(f32[1024,128]{1,0:T(8,128)} %constant.11.clone.full) | copy-start | bytes 1572868
  2.5 4.9 %collective-permute-start = (bf16[32,128]{1,0:T(8,128)(2,1)S(1)}, bf16[32,128]{1,0:T(8,128)(2,1)S(1)}, u32[]{:S(2)}, u32[]{:S(2)}) collective-permute-start(bf16[32,128]{1,0:T(8,128)(2,1)S(1)} %spectrum.1), channel_id=1, source_target_pairs={{0,2},{2,0},{1,3},{3,1},{4,6},{6,4},{5,7},{7,5},{8,10},{10,8},{9,1... | collective-permute-start | bytes 24584 | tf_op jit(solution)/shard_map/ppermute | solution.py:21
  7.4 5.2 %collective-permute-start.1 = (bf16[192,128]{1,0:T(8,128)(2,1)S(1)}, bf16[192,128]{1,0:T(8,128)(2,1)S(1)}, u32[]{:S(2)}, u32[]{:S(2)}) collective-permute-start(bf16[192,128]{1,0:T(8,128)(2,1)S(1)} %pad_maximum_fusion.1), channel_id=1, source_target_pairs={{0,8},{4,12},{8,0},{12,4},{1,9},{5,13},{9,1},{13,5},{2,10},{6,14},... | collective-permute-start | bytes 147464 | tf_op jit(solution)/shard_map/ppermute | solution.py:21
  12.6 6.0 %copy-start.1 = (f32[2,8,128]{2,1,0:T(8,128)S(1)}, f32[2,8,128]{2,1,0:T(8,128)}, u32[]{:S(2)}) copy-start(f32[2,8,128]{2,1,0:T(8,128)} %constant.8.clone.outer) | copy-start | bytes 24580
  12.6 4.7 %collective-permute-start.2 = (bf16[384,128]{1,0:T(8,128)(2,1)S(1)}, bf16[384,128]{1,0:T(8,128)(2,1)S(1)}, u32[]{:S(2)}, u32[]{:S(2)}) collective-permute-start(bf16[384,128]{1,0:T(8,128)(2,1)S(1)} %pad_maximum_fusion.own_a), channel_id=1, source_target_pairs={{0,4},{4,0},{8,12},{12,8},{1,5},{5,1},{9,13},{13,9},{2,6},{6,2},{1... | collective-permute-start | bytes 294920 | tf_op jit(solution)/shard_map/ppermute | solution.py:21
  14.4 4.2 %collective-permute-start.3 = (bf16[384,128]{1,0:T(8,128)(2,1)S(1)}, bf16[384,128]{1,0:T(8,128)(2,1)S(1)}, u32[]{:S(2)}, u32[]{:S(2)}) collective-permute-start(bf16[384,128]{1,0:T(8,128)(2,1)S(1)} %pad_maximum_fusion.own_a), channel_id=1, source_target_pairs={{0,1},{1,0},{2,3},{3,2},{4,5},{5,4},{6,7},{7,6},{8,9},{9,8},{10,11... | collective-permute-start | bytes 294920 | tf_op jit(solution)/shard_map/ppermute | solution.py:21
  17.3 1.3 %collective-permute-start.4 = (bf16[384,128]{1,0:T(8,128)(2,1)S(1)}, bf16[384,128]{1,0:T(8,128)(2,1)S(1)}, u32[]{:S(2)}, u32[]{:S(2)}) collective-permute-start(bf16[384,128]{1,0:T(8,128)(2,1)S(1)} %collective-permute-done.2.own_b), channel_id=1, source_target_pairs={{0,1},{1,0},{2,3},{3,2},{4,5},{5,4},{6,7},{7,6},{8,9},{9,8},{10,11... | collective-permute-start | bytes 294920 | tf_op jit(solution)/shard_map/ppermute | solution.py:21

commit v3 on v2

--- a/solution.py
+++ b/solution.py
@@ -10,7 +10,6 @@
 from jax.sharding import PartitionSpec as P
 
 
-HIGHEST = lax.Precision.HIGHEST
 LANES = 128
 F32 = jnp.float32
 BF16 = jnp.bfloat16
@@ -19,6 +18,11 @@
 def swapped(block, axis, distance):
     route = [(i, i ^ distance) for i in range(lax.axis_size(axis))]
     return lax.ppermute(block, axis, route)
+
+
+def two_terms(table):
+    upper = table.astype(BF16)
+    return upper, (table - upper.astype(np.float32)).astype(BF16)
 
 
 def tables(length):
@@ -28,14 +32,17 @@
     turn = 2.0 * math.pi
     outer = turn * (np.arange(rows)[:, None] * lane[None, :] % rows) / rows
     outer = np.stack([np.cos(outer), np.sin(outer)])
-    inner = turn * (lane[:, None] * lane[None, :]) / length
-    inner = np.concatenate([np.cos(inner), np.sin(inner)], axis=1)
     shift = turn * (np.arange(high)[:, None] * lane[None, :] % rows) / rows
     shift = np.stack([np.cos(shift), np.sin(shift)])
+    step = 8
+    fine = turn * (np.arange(step)[:, None] * lane[None, :]) / length
+    coarse = turn * (np.arange(0, LANES, step)[:, None] * lane[None, :]) / length
+    start = np.concatenate([np.cos(fine), np.sin(fine), np.cos(coarse), np.sin(coarse)])
     bins = np.arange(length // 2)
     full = turn * (bins[:, None] * lane[None, :] % length) / length
     full = np.concatenate([np.cos(full), np.sin(full)], axis=0)
-    return tuple(a.astype(np.float32) for a in (outer, inner, shift, full))
+    outer, shift, start, full = (a.astype(np.float32) for a in (outer, shift, start, full))
+    return outer, shift, start, np.concatenate(two_terms(full), axis=1)
 
 
 def split_two(value):
@@ -43,9 +50,16 @@
     return upper, (value - upper.astype(F32)).astype(BF16)
 
 
+def product_two(left, right):
+    upper, lower = split_two(left)
+    count, width = left.shape[0], right.shape[1] // 2
+    both = jnp.dot(jnp.concatenate([upper, lower], axis=0), right, preferred_element_type=F32)
+    small = (both[:count, width:] + both[count:, width:]) + both[count:, :width]
+    return both[:count, :width] + small
+
+
 def circulant(row):
-    spread = jnp.broadcast_to(row, (LANES, LANES))
-    return pltpu.roll(spread, 0, 1, stride=1, stride_axis=0)
+    return pltpu.roll(jnp.broadcast_to(row, (LANES, LANES)), 0, 1, stride=1, stride_axis=0)
 
 
 def keep_right():
@@ -54,21 +68,25 @@
     return q >= u
 
 
-def spectrum_kernel(strain, mask, reset, psd_ref, psd_rate, outer, inner, shift, out):
+def spectrum_kernel(strain, mask, reset, psd_ref, psd_rate, outer, shift, start, out):
     rows = strain.shape[0]
     high = psd_ref.shape[0]
     signal = strain[...] * mask[...].astype(F32)
-    left = []
-    for part in range(2):
-        for kh in range(high):
-            left.append(signal * shift[part, kh : kh + 1, :])
-    product = lax.dot_general(
-        jnp.concatenate(left, axis=0),
-        inner[...],
-        (((1,), (0,)), ((), ())),
-        precision=HIGHEST,
-        preferred_element_type=F32,
-    )
+    reference_psd = psd_ref[...]
+    rate = psd_rate[...]
+    step = start.shape[0] // 2 - LANES // 8
+    fine_c, fine_s = start[:step], start[step : 2 * step]
+    wide_c, wide_s = start[2 * step : 2 * step + LANES // 8], start[2 * step + LANES // 8 :]
+    cos_rows, sin_rows = [], []
+    for a in range(LANES // 8):
+        c, s = wide_c[a : a + 1], wide_s[a : a + 1]
+        cos_rows.append(c * fine_c - s * fine_s)
+        sin_rows.append(s * fine_c + c * fine_s)
+    cos_all, sin_all = jnp.concatenate(cos_rows, axis=0), jnp.concatenate(sin_rows, axis=0)
+    terms = [split_two(v) for v in (cos_all, sin_all)]
+    inner = jnp.concatenate([terms[0][0], terms[1][0], terms[0][1], terms[1][1]], axis=1)
+    left = [signal * shift[i, k : k + 1] for i in range(2) for k in range(high)]
+    product = product_two(jnp.concatenate(left, axis=0), inner)
     cos_one, sin_one = outer[0], outer[1]
     real_rows, imag_rows = [], []
     for kh in range(high):
@@ -80,8 +98,6 @@
         imag_rows.append(jnp.sum(sin_one * cos_sum + cos_one * sin_sum, axis=0, keepdims=True))
     real_part = jnp.concatenate(real_rows, axis=0)
     imag_part = jnp.concatenate(imag_rows, axis=0)
-    reference_psd = psd_ref[...]
-    rate = psd_rate[...]
     power = (real_part * real_part + imag_part * imag_part) / (rows * LANES / 2)
     log_power = jnp.log(power + 0.1 * reference_psd)
     keep = (1.0 - rate) * (1.0 - 0.5 * reset[0].astype(F32))
@@ -124,22 +140,22 @@
         lag = jnp.zeros((1, 1), F32)
         for part in range(2):
             row = series[b, part : part + 1, :]
+            lag = lag + jnp.sum(row * row, axis=1, keepdims=True)
             fill = jnp.zeros((1, 3 * LANES - row.shape[1]), F32)
             row = jnp.concatenate([row, fill], axis=1)
-            lag = lag + jnp.sum(row * row, axis=1, keepdims=True)
             before = jnp.zeros((LANES, LANES), F32)
             for d in range(3):
                 now = circulant(row[:, d * LANES : (d + 1) * LANES])
                 upper, lower = split_two(jnp.where(right, now, before))
-                upper_out[b, part * LANES : (part + 1) * LANES, d * LANES : (d + 1) * LANES] = upper
-                lower_out[b, part * LANES : (part + 1) * LANES, d * LANES : (d + 1) * LANES] = lower
+                upper_out[b, d, part * LANES : (part + 1) * LANES] = upper
+                lower_out[b, d, part * LANES : (part + 1) * LANES] = lower
                 before = now
         lag_out[b] = jnp.broadcast_to(lag, (8, LANES))
 
 
 def output_kernel(
     own_a, own_b, other_a, other_b, full, outer, band_up, band_low, lag,
-    snr_out, chi_out, spec, logs, toeplitz, *, order, tms, length, taps, window,
+    snr_out, chi_out, spec, logs, *, order, tms, length, taps, window,
 ):
     rows = length // LANES
     high = length // 2 // LANES
@@ -195,43 +211,51 @@
     bin_row = lax.broadcasted_iota(jnp.int32, (high, LANES), 0)
     bin_lane = lax.broadcasted_iota(jnp.int32, (high, LANES), 1)
     weight = jnp.where(bin_row + bin_lane == 0, 1.0 / length, 2.0 / length).astype(F32)
+    top_row = lax.broadcasted_iota(jnp.int32, (rows, LANES), 0) == 0
     left = []
     for c in range(2):
+        real, imag = [], []
         for i in range(near):
             scale = jnp.exp(-0.5 * logs[c, place + i]) * weight
-            real = spec[c, place + i, :high] * scale
-            imag = spec[c, place + i, high : 2 * high] * scale
+            real.append(spec[c, place + i, :high] * scale)
+            imag.append(spec[c, place + i, high : 2 * high] * scale)
+        for i in range(near - 1):
             cos_parts, sin_parts = [], []
             for kh in range(high):
-                re = jnp.broadcast_to(real[kh : kh + 1], (rows, LANES))
-                im = jnp.broadcast_to(imag[kh : kh + 1], (rows, LANES))
+                re = jnp.broadcast_to(real[i][kh : kh + 1], (rows, LANES))
+                im = jnp.broadcast_to(imag[i][kh : kh + 1], (rows, LANES))
+                if i == 0:
+                    re = jnp.where(top_row, real[near - 1][kh : kh + 1], re)
+                    im = jnp.where(top_row, imag[near - 1][kh : kh + 1], im)
                 cos_parts.append(re * cos_one + im * sin_one)
                 sin_parts.append(im * cos_one - re * sin_one)
             left.append(jnp.concatenate(cos_parts + sin_parts, axis=1))
-    white = lax.dot_general(
-        jnp.concatenate(left, axis=0),
-        full[...],
-        (((1,), (0,)), ((), ())),
-        precision=HIGHEST,
-        preferred_element_type=F32,
-    )
+    white = product_two(jnp.concatenate(left, axis=0), full[...])
     white = white.astype(BF16).astype(F32)
 
     first_out = behind * rows - 1
     out_frames = rows + 2
     first_t = first_out - (lags - 1)
     t_frames = lags - 1 + out_frames
+    assert first_t == rows and first_t + t_frames - 1 == (near - 1) * rows
     right = keep_right()
-    for c in range(2):
-        base = c * near * rows
-        before = circulant(white[base + first_t - 1 : base + first_t])
-        for s in range(t_frames):
-            at = base + first_t + s
-            now = circulant(white[at : at + 1])
-            toeplitz[c * LANES : (c + 1) * LANES, s * LANES : (s + 1) * LANES] = jnp.where(
-                right, now, before
-            ).astype(BF16)
-            before = now
+
+    def frame(c, s):
+        at = c * (near - 1) * rows + (first_t + s) % ((near - 1) * rows)
+        return circulant(white[at : at + 1])
+
+    earlier = [
+        circulant(white[top : top + 1])
+        for top in (first_t - 1, (near - 1) * rows + first_t - 1)
+    ]
+    toeplitz = []
+    for s in range(t_frames):
+        tiles = []
+        for c in range(2):
+            now = frame(c, s)
+            tiles.append(jnp.where(right, now, earlier[c]).astype(BF16))
+            earlier[c] = now
+        toeplitz.append(jnp.concatenate(tiles, axis=0))
 
     low_half = lax.broadcasted_iota(jnp.int32, (8, LANES), 0) < 4
     low_phase = lax.broadcasted_iota(jnp.int32, (8, LANES), 0) % 4 < 2
@@ -249,73 +273,98 @@
             parts.append(ref[top : top + lag_rows])
         return jnp.concatenate(parts, axis=1)
 
-    def frames_of(g_all, row):
-        accs = []
-        for n in range(out_frames + 1):
-            acc = None
-            for a in range(lags // 2):
-                s = n - 1 + (lags - 1) - 2 * a
-                if 0 <= s < t_frames:
-                    tile = g_all[row + 8 * a : row + 8 * a + 8, s * LANES : (s + 1) * LANES]
-                    acc = tile if acc is None else acc + tile
-            accs.append(acc)
-        return [accs[n + 1] + pltpu.roll(accs[n], 4, 0) for n in range(out_frames)]
-
+    def convolved(members):
+        count = len(members)
+        filt = [conv(d) for d in members]
+        f_all = jnp.concatenate(
+            [f[top : top + 16] for top in range(0, lag_rows, 16) for f in filt], axis=0
+        )
+        accs = [[None] * (out_frames + 1) for _ in members]
+        for s in range(0, t_frames, 2):
+            both = range(s, min(s + 2, t_frames))
+            valid = [
+                (a, t, t - (lags - 2) + 2 * a)
+                for a in range(lags // 2)
+                for t in both
+                if 0 <= t - (lags - 2) + 2 * a <= out_frames
+            ]
+            low = min(a for a, _, _ in valid) // 2
+            top = max(a for a, _, _ in valid) // 2 + 1
+            g = jnp.dot(
+                f_all[low * 16 * count : top * 16 * count],
+                jnp.concatenate([toeplitz[t] for t in both], axis=1),
+                preferred_element_type=F32,
+            )
+            for a, t, n in valid:
+                for k in range(count):
+                    row = ((a // 2 - low) * count + k) * 16 + a % 2 * 8
+                    tile = g[row : row + 8, (t - s) * LANES : (t - s + 1) * LANES]
+                    accs[k][n] = tile if accs[k][n] is None else accs[k][n] + tile
+        return [
+            [acc[n + 1] + pltpu.roll(acc[n], 4, 0) for n in range(out_frames)] for acc in accs
+        ]
+
+    def outputs(pair, z, corr, power, run):
+        lag_now = jnp.where(low_half, lag[pair[0]], lag[pair[1]])
+        for n in range(rows):
+            tile = slice(8 * n, 8 * n + 8)
+            c_re = jnp.where(low_half, corr[0][tile, :LANES], corr[1][tile, :LANES])
+            c_im = jnp.where(low_half, corr[0][tile, LANES:], corr[1][tile, LANES:])
+            mid = z[n + 1]
+            turned = jnp.where(low_phase, -pltpu.roll(mid, 6, 0), pltpu.roll(mid, 2, 0))
+            cross = mid * c_re + turned * c_im
+            cross = cross + pltpu.roll(cross, 6, 0)
+            here = slice(8 * n + 8, 8 * n + 16)
+            after_it = slice(8 * n + 16, 8 * n + 24)
+            win = (run[tile, LANES:] - run[tile, :LANES] + power[n]) + (
+                run[here, LANES:] + run[after_it, :LANES]
+            )
+            energy = power[n + 1]
+            chi = (win - 2.0 * cross + energy * lag_now) / (2 * window + 1)
+            lanes = slice(n * LANES, (n + 1) * LANES)
+            for top, member in zip((0, 4), pair):
+                snr_out[member, :, lanes] = energy[top : top + 2]
+                chi_out[member, :, lanes] = chi[top : top + 2]
+
+    dims = (((1,), (1,)), ((), ()))
     for group in range(0, banks, 4):
         members = range(group, min(group + 4, banks))
-        f_all = jnp.concatenate([conv(d) for d in members], axis=0)
-        g_all = jnp.dot(f_all, toeplitz[...], preferred_element_type=F32)
+        frames = convolved(members)
+        z_all, power_all, pairs, corr_all = [], [], [], []
         for first in range(0, len(members), 2):
-            d0, d1 = members[first], members[first + 1]
-            bank0, bank1 = bank ^ order[d0], bank ^ order[d1]
-            z0 = frames_of(g_all, first * lag_rows)
-            z1 = frames_of(g_all, (first + 1) * lag_rows)
+            pairs.append([bank ^ order[d] for d in members[first : first + 2]])
+            z0, z1 = frames[first], frames[first + 1]
             z = [jnp.where(low_half, p, pltpu.roll(q, 4, 0)) for p, q in zip(z0, z1)]
             z[-1] = z[-1] * after
+            z_all.append(z)
+        for z, pair in zip(z_all, pairs):
             stacked = jnp.concatenate(
                 [jnp.concatenate(z[n : n + rows], axis=0) for n in range(3)], axis=1
             )
             up, low = split_two(stacked)
+            both = jnp.concatenate([up, low], axis=0)
+            count = up.shape[0]
             corr = []
-            for d in (d0, d1):
-                b_up = band_up[bank ^ order[d]]
-                b_low = band_low[bank ^ order[d]]
-                dims = (((1,), (1,)), ((), ()))
-                corr.append(
-                    lax.dot_general(up, b_up, dims, preferred_element_type=F32)
-                    + lax.dot_general(low, b_up, dims, preferred_element_type=F32)
-                    + lax.dot_general(up, b_low, dims, preferred_element_type=F32)
-                )
-            power = []
-            for v in z:
-                square = v * v
-                power.append(square + pltpu.roll(square, 6, 0))
-            p_up, p_low = split_two(jnp.concatenate(power, axis=0))
-            run = jnp.dot(p_up, sums, preferred_element_type=F32) + jnp.dot(
-                p_low, sums, preferred_element_type=F32
-            )
-            lag_now = jnp.where(low_half, lag[bank0], lag[bank1])
-            for n in range(rows):
-                tile = slice(8 * n, 8 * n + 8)
-                c_re = jnp.where(low_half, corr[0][tile, :LANES], corr[1][tile, :LANES])
-                c_im = jnp.where(low_half, corr[0][tile, LANES:], corr[1][tile, LANES:])
-                mid = z[n + 1]
-                turned = jnp.where(low_phase, -pltpu.roll(mid, 6, 0), pltpu.roll(mid, 2, 0))
-                cross = mid * c_re + turned * c_im
-                cross = cross + pltpu.roll(cross, 6, 0)
-                prev = slice(8 * n, 8 * n + 8)
-                here = slice(8 * n + 8, 8 * n + 16)
-                nxt = slice(8 * n + 16, 8 * n + 24)
-                win = (run[prev, LANES:] - run[prev, :LANES] + power[n]) + (
-                    run[here, LANES:] + run[nxt, :LANES]
-                )
-                energy = power[n + 1]
-                chi = (win - 2.0 * cross + energy * lag_now) / (2 * window + 1)
-                lanes = slice(n * LANES, (n + 1) * LANES)
-                snr_out[bank0, :, lanes] = energy[0:2]
-                snr_out[bank1, :, lanes] = energy[4:6]
-                chi_out[bank0, :, lanes] = chi[0:2]
-                chi_out[bank1, :, lanes] = chi[4:6]
+            for member in pair:
+                b_up = jnp.concatenate([band_up[member, d] for d in range(3)], axis=1)
+                b_low = jnp.concatenate([band_low[member, d] for d in range(3)], axis=1)
+                one = lax.dot_general(both, b_up, dims, preferred_element_type=F32)
+                two = lax.dot_general(up, b_low, dims, preferred_element_type=F32)
+                corr.append(one[:count] + one[count:] + two)
+            corr_all.append(corr)
+            squares = [v * v for v in z]
+            power_all.append([v + pltpu.roll(v, 6, 0) for v in squares])
+        stacked = jnp.concatenate([v for power in power_all for v in power], axis=0)
+        up, low = split_two(stacked)
+        run_all = jnp.dot(
+            jnp.concatenate([up, low], axis=0), sums, preferred_element_type=F32
+        )
+        count = stacked.shape[0]
+        run_all = run_all[:count] + run_all[count:]
+        step = 8 * out_frames
+        for k, pair in enumerate(pairs):
+            run = run_all[k * step : (k + 1) * step]
+            outputs(pair, z_all[k], corr_all[k], power_all[k], run)
 
 
 ON_CHIP_BYTES = 3 * 2**20
@@ -324,7 +373,7 @@
 def on_chip(*arrays):
     if sum(a.size * a.dtype.itemsize for a in arrays) > ON_CHIP_BYTES:
         return arrays
-    return [pltpu.with_memory_space_constraint(a, pltpu.VMEM) for a in arrays]
+    return [pltpu.with_memory_space_constraint(a, pltpu.VMEM) for a in map(jnp.asarray, arrays)]
 
 
 def on_chip_shape(shape, dtype):
@@ -349,7 +398,7 @@
     templ = mixing.shape[2]
     window = autocorrelation.shape[2] // 2
     lags = taps // LANES
-    outer, inner, shift, full = tables(length)
+    outer, shift, start, full = tables(length)
 
     spec = pl.pallas_call(
         spectrum_kernel,
@@ -364,8 +413,8 @@
         psd_ref.reshape(high, LANES),
         psd_rate.reshape(high, LANES),
         outer,
-        inner,
         shift,
+        start,
     )
     combined = pl.pallas_call(
         filter_kernel,
@@ -374,7 +423,7 @@
         out_specs=VMEM,
         name="filters",
     )(filters.reshape(basis, taps), mixing.reshape(2 * templ, basis), basis_count)
-    band = on_chip_shape((banks, 2 * LANES, 3 * LANES), BF16)
+    band = on_chip_shape((banks, 3, 2 * LANES, LANES), BF16)
     band_up, band_low, lag = pl.pallas_call(
         band_kernel,
         out_shape=(band, band, pltpu.VMEM((banks, 8, LANES), F32)),
@@ -412,7 +461,6 @@
         scratch_shapes=[
             pltpu.VMEM((2, banks * tms + behind + 1, 4 * high, LANES), F32),
             pltpu.VMEM((2, banks * tms + behind + 1, high, LANES), F32),
-            pltpu.VMEM((2 * LANES, (lags + rows + 1) * LANES), BF16),
         ],
         name="outputs",
     )(*on_chip(held, far, held_other, far_other, full, outer, band_up, band_low, lag))

time: 21.6 us -> 21 us (0.972)
  Pallas kernels: 6.4 us -> 5.72 us
    pallas_call x1, Pallas kernels: 2.78 us -> 2.22 us  [body(): pl.pallas_call(functools.partial(output_kernel, order=tuple(order), tms=t...]
  transfers between devices with their start and end apart: 5 -> 5, of which waited for: 2 -> 2; matrix products, arithmetic and copies ran while one was open for 0% -> 0% of each run, Pallas kernels for 11% -> 12%
where the time goes in v3:
time: 21 us; the launch traced here: 20.7 us
  starting transfers between devices  7.71 us (37%)
  Pallas kernels  5.72 us (27%)
  waiting for transfers between devices  5.19 us (25%)
  between operations  2.06 us (10%)
    ppermute x5, starting transfers between devices, swapped(): return lax.ppermute(block, axis, route)  7.71 us
    ppermute x5, waiting for transfers between devices, swapped(): return lax.ppermute(block, axis, route)  5.19 us
    pallas_call x1, Pallas kernels, body(): pl.pallas_call(functools.partial(output_kernel, order=tuple(order), tms=t...  2.22 us
    pallas_call x1, Pallas kernels, body(): pl.pallas_call(band_kernel, out_shape=(band, band, pltpu.VMEM((banks, 8,...  1.28 us
    pallas_call x1, Pallas kernels, body(): pl.pallas_call(filter_kernel, out_shape=pltpu.VMEM((2 * templ * lags, LAN...  1.17 us
    pallas_call x1, Pallas kernels, body(): pl.pallas_call(spectrum_kernel, out_shape=pltpu.VMEM((8 * high, LANES), B...  1.05 us
  transfers between devices with their start and end apart: 5, of which 2 were waited for; matrix products, arithmetic and copies ran while one was open for 0% of the time, Pallas kernels for 12%

profile of v3, /device:TPU:0, one launch (start us, length us, event | category | flops | bytes accessed | tf_op | source)
XLA Modules:
  0.0 20.7 jit_solution(13459647455823875360)
XLA Ops:
  0.6 0.0 copy-start
  1.3 1.0 %spectrum.1 = bf16[32,128]{1,0:T(8,128)(2,1)S(1)} custom-call(f32[8,128]{1,0:T(8,128)} %bitcast.7, s32[8,128]{1,0:T(8,128)} %bitcast.8, s32[1]{0:T(128)S(6)} %copy.15.reset, f32[4,128]{1,0:T(4,128)} %bitcast.9, f32[4,128]{1,0:T(4,128)} %bitcast.10, f32[2,8,128]{2,1,0:T(8,128)} %constant.8.clone.outer, f32[2,4,128]{2,1,0:T(4,128)} %constant.9.clone.shift, ...), custom_call_target="tpu_custom_call" | custom-call | tf_op jit(solution)/shard_map/spectrum/pallas_call | solution.py:403
  2.4 3.0 %collective-permute-start = (bf16[32,128]{1,0:T(8,128)(2,1)S(1)}, bf16[32,128]{1,0:T(8,128)(2,1)S(1)}, u32[]{:S(2)}, u32[]{:S(2)}) collective-permute-start(bf16[32,128]{1,0:T(8,128)(2,1)S(1)} %spectrum.1), channel_id=1, source_target_pairs={{0,2},{2,0},{1,3},{3,1},{4,6},{6,4},{5,7},{7,5},{8,10},{10,8},{9,1... | collective-permute-start | bytes 24584 | tf_op jit(solution)/shard_map/ppermute | solution.py:20
  6.1 1.2 %filters.1 = bf16[128,128]{1,0:T(8,128)(2,1)S(1)} custom-call(bf16[32,2048]{1,0:T(8,128)(2,1)} %bitcast.6, bf16[8,32]{1,0:T(8,128)(2,1)} %bitcast.11, s32[1]{0:T(128)S(6)} %copy.16.count), custom_call_target="tpu_custom_call" | custom-call | tf_op jit(solution)/shard_map/filters/pallas_call | solution.py:419
  7.3 0.0 collective-permute-done
  7.3 2.9 %collective-permute-start.1 = (bf16[192,128]{1,0:T(8,128)(2,1)S(1)}, bf16[192,128]{1,0:T(8,128)(2,1)S(1)}, u32[]{:S(2)}, u32[]{:S(2)}) collective-permute-start(bf16[192,128]{1,0:T(8,128)(2,1)S(1)} %pad_maximum_fusion.1), channel_id=1, source_target_pairs={{0,8},{4,12},{8,0},{12,4},{1,9},{5,13},{9,1},{13,5},{2,10},{6,14},... | collective-permute-start | bytes 147464 | tf_op jit(solution)/shard_map/ppermute | solution.py:20
  10.2 2.3 %collective-permute-done.1 = bf16[192,128]{1,0:T(8,128)(2,1)S(1)} collective-permute-done((bf16[192,128]{1,0:T(8,128)(2,1)S(1)}, bf16[192,128]{1,0:T(8,128)(2,1)S(1)}, u32[]{:S(2)}, u32[]{:S(2)}) %collective-permute-start.1) | collective-permute-done | bytes 49184 | tf_op jit(solution)/shard_map/ppermute | solution.py:20
  12.5 0.0 copy-start.1
  12.5 1.8 %collective-permute-start.2 = (bf16[384,128]{1,0:T(8,128)(2,1)S(1)}, bf16[384,128]{1,0:T(8,128)(2,1)S(1)}, u32[]{:S(2)}, u32[]{:S(2)}) collective-permute-start(bf16[384,128]{1,0:T(8,128)(2,1)S(1)} %pad_maximum_fusion.own_a), channel_id=1, source_target_pairs={{0,4},{4,0},{8,12},{12,8},{1,5},{5,1},{9,13},{13,9},{2,6},{6,2},{1... | collective-permute-start | bytes 294920 | tf_op jit(solution)/shard_map/ppermute | solution.py:20
  14.3 0.0 collective-permute-start.3
  14.3 2.9 %collective-permute-done.2.own_b = bf16[384,128]{1,0:T(8,128)(2,1)S(1)} collective-permute-done((bf16[384,128]{1,0:T(8,128)(2,1)S(1)}, bf16[384,128]{1,0:T(8,128)(2,1)S(1)}, u32[]{:S(2)}, u32[]{:S(2)}) %collective-permute-start.2) | collective-permute-done | bytes 98336 | tf_op jit(solution)/shard_map/ppermute | solution.py:20
  17.2 0.0 collective-permute-start.4
  17.2 1.3 %bands.1 = (bf16[4,3,256,128]{3,2,1,0:T(8,128)(2,1)S(1)}, bf16[4,3,256,128]{3,2,1,0:T(8,128)(2,1)S(1)}, f32[4,8,128]{2,1,0:T(8,128)S(1)}) custom-call(f32[4,2,257]{2,1,0:T(2,128)} %series.1), custom_call_target="tpu_custom_call" | custom-call | tf_op jit(solution)/shard_map/bands/pallas_call | solution.py:427
  18.4 0.0 collective-permute-done.3.other_a
  18.5 0.0 collective-permute-done.4.other_b
  18.5 0.0 copy-done
  18.5 0.0 copy-done.1
  18.5 2.2 %outputs.1 = (f32[4,2,1024]{2,1,0:T(2,128)}, f32[4,2,1024]{2,1,0:T(2,128)}) custom-call(bf16[384,128]{1,0:T(8,128)(2,1)S(1)} %pad_maximum_fusion.own_a, bf16[384,128]{1,0:T(8,128)(2,1)S(1)} %collective-permute-done.2.own_b, bf16[384,128]{1,0:T(8,128)(2,1)S(1)} %collective-permute-done.3.other_a, bf16[384,128]{1,0:T(8,128)(2,1)S(1)} %collective-permute-done.4.other_b, ...), custom_call_target="tpu_custom_call" | custom-call | tf_op jit(solution)/shard_map/outputs/pallas_call | solution.py:454
  (2 shorter events, 0.0 us)
Async XLA Ops:
  0.6 17.8 %copy-start = (bf16[1024,256]{1,0:T(8,128)(2,1)S(1)}, bf16[1024,256]{1,0:T(8,128)(2,1)}, u32[]{:S(2)}) copy-start(bf16[1024,256]{1,0:T(8,128)(2,1)} %constant.11.clone.full) | copy-start | bytes 1572868
  2.4 4.9 %collective-permute-start = (bf16[32,128]{1,0:T(8,128)(2,1)S(1)}, bf16[32,128]{1,0:T(8,128)(2,1)S(1)}, u32[]{:S(2)}, u32[]{:S(2)}) collective-permute-start(bf16[32,128]{1,0:T(8,128)(2,1)S(1)} %spectrum.1), channel_id=1, source_target_pairs={{0,2},{2,0},{1,3},{3,1},{4,6},{6,4},{5,7},{7,5},{8,10},{10,8},{9,1... | collective-permute-start | bytes 24584 | tf_op jit(solution)/shard_map/ppermute | solution.py:20
  7.3 5.2 %collective-permute-start.1 = (bf16[192,128]{1,0:T(8,128)(2,1)S(1)}, bf16[192,128]{1,0:T(8,128)(2,1)S(1)}, u32[]{:S(2)}, u32[]{:S(2)}) collective-permute-start(bf16[192,128]{1,0:T(8,128)(2,1)S(1)} %pad_maximum_fusion.1), channel_id=1, source_target_pairs={{0,8},{4,12},{8,0},{12,4},{1,9},{5,13},{9,1},{13,5},{2,10},{6,14},... | collective-permute-start | bytes 147464 | tf_op jit(solution)/shard_map/ppermute | solution.py:20
  12.5 6.0 %copy-start.1 = (f32[2,8,128]{2,1,0:T(8,128)S(1)}, f32[2,8,128]{2,1,0:T(8,128)}, u32[]{:S(2)}) copy-start(f32[2,8,128]{2,1,0:T(8,128)} %constant.8.clone.outer) | copy-start | bytes 24580
  12.5 4.7 %collective-permute-start.2 = (bf16[384,128]{1,0:T(8,128)(2,1)S(1)}, bf16[384,128]{1,0:T(8,128)(2,1)S(1)}, u32[]{:S(2)}, u32[]{:S(2)}) collective-permute-start(bf16[384,128]{1,0:T(8,128)(2,1)S(1)} %pad_maximum_fusion.own_a), channel_id=1, source_target_pairs={{0,4},{4,0},{8,12},{12,8},{1,5},{5,1},{9,13},{13,9},{2,6},{6,2},{1... | collective-permute-start | bytes 294920 | tf_op jit(solution)/shard_map/ppermute | solution.py:20
  14.3 4.2 %collective-permute-start.3 = (bf16[384,128]{1,0:T(8,128)(2,1)S(1)}, bf16[384,128]{1,0:T(8,128)(2,1)S(1)}, u32[]{:S(2)}, u32[]{:S(2)}) collective-permute-start(bf16[384,128]{1,0:T(8,128)(2,1)S(1)} %pad_maximum_fusion.own_a), channel_id=1, source_target_pairs={{0,1},{1,0},{2,3},{3,2},{4,5},{5,4},{6,7},{7,6},{8,9},{9,8},{10,11... | collective-permute-start | bytes 294920 | tf_op jit(solution)/shard_map/ppermute | solution.py:20
  17.2 1.3 %collective-permute-start.4 = (bf16[384,128]{1,0:T(8,128)(2,1)S(1)}, bf16[384,128]{1,0:T(8,128)(2,1)S(1)}, u32[]{:S(2)}, u32[]{:S(2)}) collective-permute-start(bf16[384,128]{1,0:T(8,128)(2,1)S(1)} %collective-permute-done.2.own_b), channel_id=1, source_target_pairs={{0,1},{1,0},{2,3},{3,2},{4,5},{5,4},{6,7},{7,6},{8,9},{9,8},{10,11... | collective-permute-start | bytes 294920 | tf_op jit(solution)/shard_map/ppermute | solution.py:20

commit v4 on v3

--- a/solution.py
+++ b/solution.py
@@ -16,8 +16,14 @@
 
 
 def swapped(block, axis, distance):
-    route = [(i, i ^ distance) for i in range(lax.axis_size(axis))]
-    return lax.ppermute(block, axis, route)
+    count = lax.axis_size("rate")
+    places = range(lax.axis_size(axis) * count)
+    route = [(i, (i // count ^ distance) * count + (i % count ^ 1)) for i in places]
+    return lax.ppermute(block, (axis, "rate"), route)
+
+
+def swapped_cores(block):
+    return lax.ppermute(block, "rate", [(i, i ^ 1) for i in range(lax.axis_size("rate"))])
 
 
 def two_terms(table):
@@ -155,7 +161,7 @@
 
 def output_kernel(
     own_a, own_b, other_a, other_b, full, outer, band_up, band_low, lag,
-    snr_out, chi_out, spec, logs, *, order, tms, length, taps, window,
+    snr_out, chi_out, spec, logs, *, slots, tms, length, taps, window,
 ):
     rows = length // LANES
     high = length // 2 // LANES
@@ -163,10 +169,10 @@
     lags = taps // LANES
     lag_rows = lags * 4
     piece_rows = tms * spec_rows + 2 * lag_rows
-    pieces = len(order) * tms
+    pieces = len(slots) * tms
     behind = -(-(taps + window) // length)
     near = behind + 2
-    banks = len(order)
+    banks = len(slots)
     half = banks // 2
     bank = lax.axis_index("bank")
     tm = lax.axis_index("tm")
@@ -183,13 +189,14 @@
             logs[c, i] = zero[:high]
         spec[c, pieces + behind] = zero
         logs[c, pieces + behind] = zero[:high]
-        for d in range(banks):
-            ref, start = piece(c, d)
+        for k, (d, crossed) in enumerate(slots):
+            ref, start = piece(c, k)
             for e in range(tms):
                 top = start + e * spec_rows
                 value = ref[top : top + 4 * high].astype(F32)
                 value = value + ref[top + 4 * high : top + 8 * high].astype(F32)
-                spec[c, ((bank ^ order[d]) * tms + (tm ^ e)) + behind] = value
+                band = c ^ crossed ^ (e.bit_count() & 1)
+                spec[band, (bank ^ d) * tms + (tm ^ e) + behind] = value
 
     def advance(g, states):
         nexts = []
@@ -265,11 +272,12 @@
     upto = (lane_row <= lane_col).astype(BF16)
     sums = jnp.concatenate([upto, jnp.ones((LANES, LANES), BF16)], axis=1)
 
-    def conv(d):
+    def conv(k):
+        crossed = slots[k][1]
         parts = []
-        for c in range(2):
-            ref, start = piece(c, d)
-            top = start + tms * spec_rows + c * lag_rows
+        for c in (crossed, 1 - crossed):
+            ref, start = piece(c, k)
+            top = start + tms * spec_rows + (c ^ crossed) * lag_rows
             parts.append(ref[top : top + lag_rows])
         return jnp.concatenate(parts, axis=1)
 
@@ -332,7 +340,7 @@
         frames = convolved(members)
         z_all, power_all, pairs, corr_all = [], [], [], []
         for first in range(0, len(members), 2):
-            pairs.append([bank ^ order[d] for d in members[first : first + 2]])
+            pairs.append([bank ^ slots[k][0] for k in members[first : first + 2]])
             z0, z1 = frames[first], frames[first + 1]
             z = [jnp.where(low_half, p, pltpu.roll(q, 4, 0)) for p, q in zip(z0, z1)]
             z[-1] = z[-1] * after
@@ -437,23 +445,29 @@
         spec = jnp.concatenate([spec, swapped(spec, "tm", distance)])
         distance *= 2
     held = jnp.concatenate([spec, combined])
+    slots = [(0, 0)]
     distance = banks // 2
-    order = [0]
-    while distance > 1:
+    while distance > 2:
         held = jnp.concatenate([held, swapped(held, "bank", distance)])
-        order = order + [d ^ distance for d in order]
+        slots = slots + [(d ^ distance, p ^ 1) for d, p in slots]
         distance //= 2
-    far = swapped(held, "bank", 1)
-    order = order + [d ^ 1 for d in order]
-    held_other = swapped(held, "rate", 1)
-    far_other = swapped(far, "rate", 1)
+    far = swapped(held, "bank", 2)
+    near = swapped(held, "bank", 1)
+    first = jnp.concatenate([held, near])
+    last = swapped(far, "bank", 1)
+    second = jnp.concatenate([far, last])
+    slots = slots + [(d ^ 1, p ^ 1) for d, p in slots]
+    slots = slots + [(d ^ 2, p ^ 1) for d, p in slots]
+    first_other = swapped_cores(first)
+    second_other = swapped_cores(second)
 
     behind = -(-(taps + window) // length)
+    near = behind + 2
     share = templ // 2
     out = jax.ShapeDtypeStruct((banks, share, length), F32)
     return pl.pallas_call(
         functools.partial(
-            output_kernel, order=tuple(order), tms=tms, length=length, taps=taps, window=window
+            output_kernel, slots=slots, tms=tms, length=length, taps=taps, window=window
         ),
         out_shape=(out, out),
         in_specs=[VMEM] * 9,
@@ -463,7 +477,7 @@
             pltpu.VMEM((2, banks * tms + behind + 1, high, LANES), F32),
         ],
         name="outputs",
-    )(*on_chip(held, far, held_other, far_other, full, outer, band_up, band_low, lag))
+    )(*on_chip(first, second, first_other, second_other, full, outer, band_up, band_low, lag))
 
 
 def solution(mesh):

time: 21 us -> 22.2 us (1.057)
  waiting for transfers between devices: 5.19 us -> 6.78 us
  starting transfers between devices: 7.71 us -> 7.35 us
    ppermute x5 -> x6, waiting for transfers between devices: 5.19 us -> 6.78 us  [the longest x4 6.77 us: swapped(): return lax.ppermute(block, (axis, 'rate'), route)]
    ppermute x5 -> x6, starting transfers between devices: 7.71 us -> 7.35 us  [the longest x4 6.7 us: swapped(): return lax.ppermute(block, (axis, 'rate'), route)]
  transfers between devices with their start and end apart: 5 -> 6, of which waited for: 2 -> 2; matrix products, arithmetic and copies ran while one was open for 0% -> 0% of each run, Pallas kernels for 12% -> 11%
where the time goes in v4:
time: 22.2 us; the launch traced here: 22 us
  starting transfers between devices  7.35 us (33%)
  waiting for transfers between devices  6.78 us (31%)
  Pallas kernels  5.73 us (26%)
  between operations  2.07 us (9%)
    ppermute x4, waiting for transfers between devices, swapped(): return lax.ppermute(block, (axis, 'rate'), route)  6.77 us
    ppermute x4, starting transfers between devices, swapped(): return lax.ppermute(block, (axis, 'rate'), route)  6.7 us
    pallas_call x1, Pallas kernels, body(): pl.pallas_call(functools.partial(output_kernel, slots=slots, tms=tms, len...  2.23 us
    pallas_call x1, Pallas kernels, body(): pl.pallas_call(band_kernel, out_shape=(band, band, pltpu.VMEM((banks, 8,...  1.28 us
    pallas_call x1, Pallas kernels, body(): pl.pallas_call(filter_kernel, out_shape=pltpu.VMEM((2 * templ * lags, LAN...  1.17 us
    pallas_call x1, Pallas kernels, body(): pl.pallas_call(spectrum_kernel, out_shape=pltpu.VMEM((8 * high, LANES), B...  1.05 us
    ppermute x2, starting transfers between devices, swapped_cores(): lax.ppermute(block, 'rate', [(i, i ^ 1) for i in range(lax.axis_size('rat...  0.65 us
  transfers between devices with their start and end apart: 6, of which 2 were waited for; matrix products, arithmetic and copies ran while one was open for 0% of the time, Pallas kernels for 11%

profile of v4, /device:TPU:0, one launch (start us, length us, event | category | flops | bytes accessed | tf_op | source)
XLA Modules:
  0.0 22.0 jit_solution(5659669489581625293)
XLA Ops:
  0.6 0.0 copy-start
  1.3 1.0 %spectrum.1 = bf16[32,128]{1,0:T(8,128)(2,1)S(1)} custom-call(f32[8,128]{1,0:T(8,128)} %bitcast.7, s32[8,128]{1,0:T(8,128)} %bitcast.8, s32[1]{0:T(128)S(6)} %copy.16.reset, f32[4,128]{1,0:T(4,128)} %bitcast.9, f32[4,128]{1,0:T(4,128)} %bitcast.10, f32[2,8,128]{2,1,0:T(8,128)} %constant.8.clone.outer, f32[2,4,128]{2,1,0:T(4,128)} %constant.9.clone.shift, ...), custom_call_target="tpu_custom_call" | custom-call | tf_op jit(solution)/shard_map/spectrum/pallas_call | solution.py:411
  2.4 2.5 %collective-permute-start = (bf16[32,128]{1,0:T(8,128)(2,1)S(1)}, bf16[32,128]{1,0:T(8,128)(2,1)S(1)}, u32[]{:S(2)}, u32[]{:S(2)}) collective-permute-start(bf16[32,128]{1,0:T(8,128)(2,1)S(1)} %spectrum.1), channel_id=1, source_target_pairs={{0,3},{1,2},{2,1},{3,0},{4,7},{5,6},{6,5},{7,4},{8,11},{9,10},{10,... | collective-permute-start | bytes 24584 | tf_op jit(solution)/shard_map/ppermute | solution.py:22
  5.5 1.2 %filters.1 = bf16[128,128]{1,0:T(8,128)(2,1)S(1)} custom-call(bf16[32,2048]{1,0:T(8,128)(2,1)} %bitcast.6, bf16[8,32]{1,0:T(8,128)(2,1)} %bitcast.11, s32[1]{0:T(128)S(6)} %copy.17.count), custom_call_target="tpu_custom_call" | custom-call | tf_op jit(solution)/shard_map/filters/pallas_call | solution.py:427
  6.7 0.0 collective-permute-done
  6.7 1.9 %collective-permute-start.1 = (bf16[192,128]{1,0:T(8,128)(2,1)S(1)}, bf16[192,128]{1,0:T(8,128)(2,1)S(1)}, u32[]{:S(2)}, u32[]{:S(2)}) collective-permute-start(bf16[192,128]{1,0:T(8,128)(2,1)S(1)} %pad_maximum_fusion.1), channel_id=1, source_target_pairs={{0,5},{1,4},{4,1},{5,0},{8,13},{9,12},{12,9},{13,8},{2,7},{3,6},{6... | collective-permute-start | bytes 147464 | tf_op jit(solution)/shard_map/ppermute | solution.py:22
  8.6 2.3 %collective-permute-start.2 = (bf16[192,128]{1,0:T(8,128)(2,1)S(1)}, bf16[192,128]{1,0:T(8,128)(2,1)S(1)}, u32[]{:S(2)}, u32[]{:S(2)}) collective-permute-start(bf16[192,128]{1,0:T(8,128)(2,1)S(1)} %pad_maximum_fusion.1), channel_id=1, source_target_pairs={{0,9},{1,8},{4,13},{5,12},{8,1},{9,0},{12,5},{13,4},{2,11},{3,10},... | collective-permute-start | bytes 147464 | tf_op jit(solution)/shard_map/ppermute | solution.py:22
  10.9 0.0 collective-permute-done.1
  11.0 0.5 %collective-permute-start.4 = (bf16[384,128]{1,0:T(8,128)(2,1)S(1)}, bf16[384,128]{1,0:T(8,128)(2,1)S(1)}, u32[]{:S(2)}, u32[]{:S(2)}) collective-permute-start(bf16[384,128]{1,0:T(8,128)(2,1)S(1)} %pad_maximum_fusion.own_a), channel_id=1, source_target_pairs={{0,1},{1,0},{2,3},{3,2},{4,5},{5,4},{6,7},{7,6},{8,9},{9,8},{10,11... | collective-permute-start | bytes 294920 | tf_op jit(solution)/shard_map/ppermute | solution.py:26
  11.4 3.0 %collective-permute-done.2 = bf16[192,128]{1,0:T(8,128)(2,1)S(1)} collective-permute-done((bf16[192,128]{1,0:T(8,128)(2,1)S(1)}, bf16[192,128]{1,0:T(8,128)(2,1)S(1)}, u32[]{:S(2)}, u32[]{:S(2)}) %collective-permute-start.2) | collective-permute-done | bytes 49184 | tf_op jit(solution)/shard_map/ppermute | solution.py:22
  14.5 0.0 collective-permute-start.3
  14.5 3.7 %collective-permute-done.3 = bf16[192,128]{1,0:T(8,128)(2,1)S(1)} collective-permute-done((bf16[192,128]{1,0:T(8,128)(2,1)S(1)}, bf16[192,128]{1,0:T(8,128)(2,1)S(1)}, u32[]{:S(2)}, u32[]{:S(2)}) %collective-permute-start.3) | collective-permute-done | bytes 49184 | tf_op jit(solution)/shard_map/ppermute | solution.py:22
  18.2 0.0 copy-start.1
  18.2 0.2 collective-permute-start.5
  18.4 1.3 %bands.1 = (bf16[4,3,256,128]{3,2,1,0:T(8,128)(2,1)S(1)}, bf16[4,3,256,128]{3,2,1,0:T(8,128)(2,1)S(1)}, f32[4,8,128]{2,1,0:T(8,128)S(1)}) custom-call(f32[4,2,257]{2,1,0:T(2,128)} %series.1), custom_call_target="tpu_custom_call" | custom-call | tf_op jit(solution)/shard_map/bands/pallas_call | solution.py:435
  19.7 0.0 collective-permute-done.4.other_a
  19.7 0.0 collective-permute-done.5.other_b
  19.7 0.0 copy-done
  19.7 0.0 copy-done.1
  19.7 2.2 %outputs.1 = (f32[4,2,1024]{2,1,0:T(2,128)}, f32[4,2,1024]{2,1,0:T(2,128)}) custom-call(bf16[384,128]{1,0:T(8,128)(2,1)S(1)} %pad_maximum_fusion.own_a, bf16[384,128]{1,0:T(8,128)(2,1)S(1)} %constant_dynamic-update-slice_fusion.own_b, bf16[384,128]{1,0:T(8,128)(2,1)S(1)} %collective-permute-done.4.other_a, ...), custom_call_target="tpu_custom_call" | custom-call | tf_op jit(solution)/shard_map/outputs/pallas_call | solution.py:468
  (4 shorter events, 0.0 us)
Async XLA Ops:
  0.6 19.1 %copy-start = (bf16[1024,256]{1,0:T(8,128)(2,1)S(1)}, bf16[1024,256]{1,0:T(8,128)(2,1)}, u32[]{:S(2)}) copy-start(bf16[1024,256]{1,0:T(8,128)(2,1)} %constant.11.clone.full) | copy-start | bytes 1572868
  2.4 4.3 %collective-permute-start = (bf16[32,128]{1,0:T(8,128)(2,1)S(1)}, bf16[32,128]{1,0:T(8,128)(2,1)S(1)}, u32[]{:S(2)}, u32[]{:S(2)}) collective-permute-start(bf16[32,128]{1,0:T(8,128)(2,1)S(1)} %spectrum.1), channel_id=1, source_target_pairs={{0,3},{1,2},{2,1},{3,0},{4,7},{5,6},{6,5},{7,4},{8,11},{9,10},{10,... | collective-permute-start | bytes 24584 | tf_op jit(solution)/shard_map/ppermute | solution.py:22
  6.7 4.2 %collective-permute-start.1 = (bf16[192,128]{1,0:T(8,128)(2,1)S(1)}, bf16[192,128]{1,0:T(8,128)(2,1)S(1)}, u32[]{:S(2)}, u32[]{:S(2)}) collective-permute-start(bf16[192,128]{1,0:T(8,128)(2,1)S(1)} %pad_maximum_fusion.1), channel_id=1, source_target_pairs={{0,5},{1,4},{4,1},{5,0},{8,13},{9,12},{12,9},{13,8},{2,7},{3,6},{6... | collective-permute-start | bytes 147464 | tf_op jit(solution)/shard_map/ppermute | solution.py:22
  8.6 5.8 %collective-permute-start.2 = (bf16[192,128]{1,0:T(8,128)(2,1)S(1)}, bf16[192,128]{1,0:T(8,128)(2,1)S(1)}, u32[]{:S(2)}, u32[]{:S(2)}) collective-permute-start(bf16[192,128]{1,0:T(8,128)(2,1)S(1)} %pad_maximum_fusion.1), channel_id=1, source_target_pairs={{0,9},{1,8},{4,13},{5,12},{8,1},{9,0},{12,5},{13,4},{2,11},{3,10},... | collective-permute-start | bytes 147464 | tf_op jit(solution)/shard_map/ppermute | solution.py:22
  11.0 8.7 %collective-permute-start.4 = (bf16[384,128]{1,0:T(8,128)(2,1)S(1)}, bf16[384,128]{1,0:T(8,128)(2,1)S(1)}, u32[]{:S(2)}, u32[]{:S(2)}) collective-permute-start(bf16[384,128]{1,0:T(8,128)(2,1)S(1)} %pad_maximum_fusion.own_a), channel_id=1, source_target_pairs={{0,1},{1,0},{2,3},{3,2},{4,5},{5,4},{6,7},{7,6},{8,9},{9,8},{10,11... | collective-permute-start | bytes 294920 | tf_op jit(solution)/shard_map/ppermute | solution.py:26
  14.5 3.7 %collective-permute-start.3 = (bf16[192,128]{1,0:T(8,128)(2,1)S(1)}, bf16[192,128]{1,0:T(8,128)(2,1)S(1)}, u32[]{:S(2)}, u32[]{:S(2)}) collective-permute-start(bf16[192,128]{1,0:T(8,128)(2,1)S(1)} %collective-permute-done.2), channel_id=1, source_target_pairs={{0,5},{1,4},{4,1},{5,0},{8,13},{9,12},{12,9},{13,8},{2,7},{3,6},{6... | collective-permute-start | bytes 147464 | tf_op jit(solution)/shard_map/ppermute | solution.py:22
  18.2 1.5 %copy-start.1 = (f32[2,8,128]{2,1,0:T(8,128)S(1)}, f32[2,8,128]{2,1,0:T(8,128)}, u32[]{:S(2)}) copy-start(f32[2,8,128]{2,1,0:T(8,128)} %constant.8.clone.outer) | copy-start | bytes 24580
  18.2 1.5 %collective-permute-start.5 = (bf16[384,128]{1,0:T(8,128)(2,1)S(1)}, bf16[384,128]{1,0:T(8,128)(2,1)S(1)}, u32[]{:S(2)}, u32[]{:S(2)}) collective-permute-start(bf16[384,128]{1,0:T(8,128)(2,1)S(1)} %constant_dynamic-update-slice_fusion.own_b), channel_id=1, source_target_pairs={{0,1},{1,0},{2,3},{3,2},{4,5},{5,4},{6,7},{7,6},{8,9},{9,8},{10,11... | collective-permute-start | bytes 294920 | tf_op jit(solution)/shard_map/ppermute | solution.py:26

commit v5 on v4

--- a/solution.py
+++ b/solution.py
@@ -74,12 +74,12 @@
     return q >= u
 
 
-def spectrum_kernel(strain, mask, reset, psd_ref, psd_rate, outer, shift, start, out):
+def spectrum_kernel(strain, mask, reset, psd_ref, psd_rate, outer, shift, start, out, levels):
     rows = strain.shape[0]
     high = psd_ref.shape[0]
+    levels[:high] = psd_ref[...]
+    levels[high:] = psd_rate[...]
     signal = strain[...] * mask[...].astype(F32)
-    reference_psd = psd_ref[...]
-    rate = psd_rate[...]
     step = start.shape[0] // 2 - LANES // 8
     fine_c, fine_s = start[:step], start[step : 2 * step]
     wide_c, wide_s = start[2 * step : 2 * step + LANES // 8], start[2 * step + LANES // 8 :]
@@ -104,15 +104,12 @@
         imag_rows.append(jnp.sum(sin_one * cos_sum + cos_one * sin_sum, axis=0, keepdims=True))
     real_part = jnp.concatenate(real_rows, axis=0)
     imag_part = jnp.concatenate(imag_rows, axis=0)
-    power = (real_part * real_part + imag_part * imag_part) / (rows * LANES / 2)
-    log_power = jnp.log(power + 0.1 * reference_psd)
-    keep = (1.0 - rate) * (1.0 - 0.5 * reset[0].astype(F32))
-    first = (lax.axis_index("bank") == 0) & (lax.axis_index("tm") == 0)
-    drive = rate * log_power + jnp.where(first, keep * jnp.log(reference_psd), 0.0)
-    whole = jnp.concatenate([real_part, imag_part, drive, keep], axis=0)
-    upper, lower = split_two(whole)
-    out[: 4 * high] = upper
-    out[4 * high :] = lower
+    row = lax.broadcasted_iota(jnp.int32, imag_part.shape, 0)
+    lane = lax.broadcasted_iota(jnp.int32, imag_part.shape, 1)
+    imag_part = jnp.where(row + lane == 0, reset[0].astype(F32), imag_part)
+    upper, lower = split_two(jnp.concatenate([real_part, imag_part], axis=0))
+    out[: 2 * high] = upper
+    out[2 * high :] = lower
 
 
 def filter_kernel(filters, mixing, count, out):
@@ -140,7 +137,12 @@
     out[...] = jnp.concatenate(own + other, axis=0).astype(BF16)
 
 
-def band_kernel(series, upper_out, lower_out, lag_out):
+def band_kernel(series, levels, levels_other, upper_out, lower_out, lag_out, levels_out):
+    high = levels.shape[0] // 2
+    for c, ref in enumerate((levels, levels_other)):
+        reference_psd, rate = ref[:high], ref[high:]
+        for k, value in enumerate((0.1 * reference_psd, jnp.log(reference_psd), rate)):
+            levels_out[c, k] = jnp.concatenate([value, value], axis=0)
     right = keep_right()
     for b in range(series.shape[0]):
         lag = jnp.zeros((1, 1), F32)
@@ -160,12 +162,12 @@
 
 
 def output_kernel(
-    own_a, own_b, other_a, other_b, full, outer, band_up, band_low, lag,
-    snr_out, chi_out, spec, logs, *, slots, tms, length, taps, window,
+    own_a, own_b, other_a, other_b, full, outer, band_up, band_low, lag, levels,
+    snr_out, chi_out, spec, drives, keeps, logs, *, slots, tms, length, taps, window,
 ):
     rows = length // LANES
     high = length // 2 // LANES
-    spec_rows = 8 * high
+    spec_rows = 4 * high
     lags = taps // LANES
     lag_rows = lags * 4
     piece_rows = tms * spec_rows + 2 * lag_rows
@@ -182,32 +184,41 @@
     def piece(c, d):
         return bufs[c][d // half], (d % half) * piece_rows
 
-    zero = jnp.zeros((4 * high, LANES), F32)
+    tile_row = lax.broadcasted_iota(jnp.int32, (2 * high, LANES), 0)
+    tile_lane = lax.broadcasted_iota(jnp.int32, (2 * high, LANES), 1)
+    flag_place = (tile_row == high) & (tile_lane == 0)
+    zero = jnp.zeros((2 * high, LANES), F32)
     for c in range(2):
         for i in range(behind):
             spec[c, i] = zero
-            logs[c, i] = zero[:high]
+            logs[c, i] = zero
         spec[c, pieces + behind] = zero
-        logs[c, pieces + behind] = zero[:high]
+        logs[c, pieces + behind] = zero
         for k, (d, crossed) in enumerate(slots):
             ref, start = piece(c, k)
             for e in range(tms):
                 top = start + e * spec_rows
-                value = ref[top : top + 4 * high].astype(F32)
-                value = value + ref[top + 4 * high : top + 8 * high].astype(F32)
+                value = ref[top : top + 2 * high].astype(F32)
+                value = value + ref[top + 2 * high : top + 4 * high].astype(F32)
                 band = c ^ crossed ^ (e.bit_count() & 1)
-                spec[band, (bank ^ d) * tms + (tm ^ e) + behind] = value
+                at = (bank ^ d) * tms + (tm ^ e)
+                flag = value[high : high + 1, 0:1]
+                value = jnp.where(flag_place, 0.0, value)
+                square = value * value
+                power = (square + pltpu.roll(square, high, 0)) / (length / 2)
+                rate = levels[band, 2]
+                spec[band, at + behind] = value
+                drives[band, at] = rate * jnp.log(power + levels[band, 0])
+                keeps[band, at] = (1.0 - rate) * (1.0 - 0.5 * flag)
 
     def advance(g, states):
         nexts = []
         for c in range(2):
-            drive = spec[c, g + behind, 2 * high : 3 * high]
-            keep = spec[c, g + behind, 3 * high : 4 * high]
-            nexts.append(keep * states[c] + drive)
+            nexts.append(keeps[c, g] * states[c] + drives[c, g])
             logs[c, g + behind] = nexts[c]
         return tuple(nexts)
 
-    states = (zero[:high], zero[:high])
+    states = (levels[0, 1], levels[1, 1])
     if pieces <= 16:
         for g in range(pieces):
             states = advance(g, states)
@@ -215,17 +226,16 @@
         lax.fori_loop(0, pieces, advance, states)
 
     cos_one, sin_one = outer[0], outer[1]
-    bin_row = lax.broadcasted_iota(jnp.int32, (high, LANES), 0)
-    bin_lane = lax.broadcasted_iota(jnp.int32, (high, LANES), 1)
-    weight = jnp.where(bin_row + bin_lane == 0, 1.0 / length, 2.0 / length).astype(F32)
+    first_bin = (tile_row % high == 0) & (tile_lane == 0)
+    weight = jnp.where(first_bin, 1.0 / length, 2.0 / length).astype(F32)
     top_row = lax.broadcasted_iota(jnp.int32, (rows, LANES), 0) == 0
     left = []
     for c in range(2):
         real, imag = [], []
         for i in range(near):
-            scale = jnp.exp(-0.5 * logs[c, place + i]) * weight
-            real.append(spec[c, place + i, :high] * scale)
-            imag.append(spec[c, place + i, high : 2 * high] * scale)
+            scaled = spec[c, place + i] * (jnp.exp(-0.5 * logs[c, place + i]) * weight)
+            real.append(scaled[:high])
+            imag.append(scaled[high:])
         for i in range(near - 1):
             cos_parts, sin_parts = [], []
             for kh in range(high):
@@ -408,11 +418,14 @@
     lags = taps // LANES
     outer, shift, start, full = tables(length)
 
-    spec = pl.pallas_call(
+    spec, levels = pl.pallas_call(
         spectrum_kernel,
-        out_shape=pltpu.VMEM((8 * high, LANES), BF16),
+        out_shape=(
+            pltpu.VMEM((4 * high, LANES), BF16),
+            pltpu.VMEM((2 * high, LANES), F32),
+        ),
         in_specs=[VMEM, VMEM, SMEM] + [VMEM] * 5,
-        out_specs=VMEM,
+        out_specs=(VMEM, VMEM),
         name="spectrum",
     )(
         strain.reshape(rows, LANES),
@@ -431,15 +444,6 @@
         out_specs=VMEM,
         name="filters",
     )(filters.reshape(basis, taps), mixing.reshape(2 * templ, basis), basis_count)
-    band = on_chip_shape((banks, 3, 2 * LANES, LANES), BF16)
-    band_up, band_low, lag = pl.pallas_call(
-        band_kernel,
-        out_shape=(band, band, pltpu.VMEM((banks, 8, LANES), F32)),
-        in_specs=[VMEM],
-        out_specs=(VMEM, VMEM, VMEM),
-        name="bands",
-    )(autocorrelation)
-
     distance = 1
     while distance < tms:
         spec = jnp.concatenate([spec, swapped(spec, "tm", distance)])
@@ -454,12 +458,27 @@
     far = swapped(held, "bank", 2)
     near = swapped(held, "bank", 1)
     first = jnp.concatenate([held, near])
+    levels_other = swapped_cores(levels)
     last = swapped(far, "bank", 1)
     second = jnp.concatenate([far, last])
     slots = slots + [(d ^ 1, p ^ 1) for d, p in slots]
     slots = slots + [(d ^ 2, p ^ 1) for d, p in slots]
     first_other = swapped_cores(first)
     second_other = swapped_cores(second)
+
+    band = on_chip_shape((banks, 3, 2 * LANES, LANES), BF16)
+    band_up, band_low, lag, levels = pl.pallas_call(
+        band_kernel,
+        out_shape=(
+            band,
+            band,
+            pltpu.VMEM((banks, 8, LANES), F32),
+            pltpu.VMEM((2, 3, 2 * high, LANES), F32),
+        ),
+        in_specs=[VMEM] * 3,
+        out_specs=(VMEM,) * 4,
+        name="bands",
+    )(autocorrelation, *on_chip(levels, levels_other))
 
     behind = -(-(taps + window) // length)
     near = behind + 2
@@ -470,14 +489,16 @@
             output_kernel, slots=slots, tms=tms, length=length, taps=taps, window=window
         ),
         out_shape=(out, out),
-        in_specs=[VMEM] * 9,
+        in_specs=[VMEM] * 10,
         out_specs=(VMEM, VMEM),
         scratch_shapes=[
-            pltpu.VMEM((2, banks * tms + behind + 1, 4 * high, LANES), F32),
-            pltpu.VMEM((2, banks * tms + behind + 1, high, LANES), F32),
+            pltpu.VMEM((2, banks * tms + behind + 1, 2 * high, LANES), F32),
+            pltpu.VMEM((2, banks * tms, 2 * high, LANES), F32),
+            pltpu.VMEM((2, banks * tms, 2 * high, LANES), F32),
+            pltpu.VMEM((2, banks * tms + behind + 1, 2 * high, LANES), F32),
         ],
         name="outputs",
-    )(*on_chip(first, second, first_other, second_other, full, outer, band_up, band_low, lag))
+    )(*on_chip(first, second, first_other, second_other, full, outer, band_up, band_low, lag, levels))
 
 
 def solution(mesh):

time: 22.2 us -> 23 us (1.036)
  starting transfers between devices: 7.35 us -> 7.73 us
  waiting for transfers between devices: 6.78 us -> 7.1 us
    ppermute x2 -> x3, waiting for transfers between devices: 0.01 us -> 0.83 us  [swapped_cores(): lax.ppermute(block, 'rate', [(i, i ^ 1) for i in range(lax.axis_size('rat...]
    ppermute x4, waiting for transfers between devices: 6.77 us -> 6.27 us  [swapped(): return lax.ppermute(block, (axis, 'rate'), route)]
    ppermute x2 -> x3, starting transfers between devices: 0.65 us -> 1.11 us  [swapped_cores(): lax.ppermute(block, 'rate', [(i, i ^ 1) for i in range(lax.axis_size('rat...]
  transfers between devices with their start and end apart: 6 -> 7, of which waited for: 2 -> 3; matrix products, arithmetic and copies ran while one was open for 0% -> 0% of each run, Pallas kernels for 11% -> 11%
where the time goes in v5:
time: 23 us; the launch traced here: 22.7 us
  starting transfers between devices  7.73 us (34%)
  waiting for transfers between devices  7.1 us (31%)
  Pallas kernels  5.78 us (25%)
  between operations  2.06 us (9%)
    ppermute x4, starting transfers between devices, swapped(): return lax.ppermute(block, (axis, 'rate'), route)  6.62 us
    ppermute x4, waiting for transfers between devices, swapped(): return lax.ppermute(block, (axis, 'rate'), route)  6.27 us
    pallas_call x1, Pallas kernels, body(): pl.pallas_call(functools.partial(output_kernel, slots=slots, tms=tms, len...  2.27 us
    pallas_call x1, Pallas kernels, body(): pl.pallas_call(band_kernel, out_shape=(band, band, pltpu.VMEM((banks, 8,...  1.29 us
    pallas_call x1, Pallas kernels, body(): pl.pallas_call(filter_kernel, out_shape=pltpu.VMEM((2 * templ * lags, LAN...  1.17 us
    ppermute x3, starting transfers between devices, swapped_cores(): lax.ppermute(block, 'rate', [(i, i ^ 1) for i in range(lax.axis_size('rat...  1.11 us
    pallas_call x1, Pallas kernels, body(): pl.pallas_call(spectrum_kernel, out_shape=(pltpu.VMEM((4 * high, LANES),...  1.04 us
    ppermute x3, waiting for transfers between devices, swapped_cores(): lax.ppermute(block, 'rate', [(i, i ^ 1) for i in range(lax.axis_size('rat...  0.83 us
  transfers between devices with their start and end apart: 7, of which 3 were waited for; matrix products, arithmetic and copies ran while one was open for 0% of the time, Pallas kernels for 11%

profile of v5, /device:TPU:0, one launch (start us, length us, event | category | flops | bytes accessed | tf_op | source)
XLA Modules:
  0.0 22.7 jit_solution(1811961871023586037)
XLA Ops:
  0.6 0.0 copy-start
  1.3 1.0 %spectrum.1 = (bf16[16,128]{1,0:T(8,128)(2,1)S(1)}, f32[8,128]{1,0:T(8,128)S(1)}) custom-call(f32[8,128]{1,0:T(8,128)} %bitcast.7, s32[8,128]{1,0:T(8,128)} %bitcast.8, s32[1]{0:T(128)S(6)} %copy.16.reset, f32[4,128]{1,0:T(4,128)} %bitcast.9, f32[4,128]{1,0:T(4,128)} %bitcast.10, f32[2,8,128]{2,1,0:T(8,128)} %constant.8.clone.outer, ...), custom_call_target="tpu_custom_call" | custom-call | tf_op jit(solution)/shard_map/spectrum/pallas_call | solution.py:421
  2.4 2.5 %collective-permute-start = (bf16[16,128]{1,0:T(8,128)(2,1)S(1)}, bf16[16,128]{1,0:T(8,128)(2,1)S(1)}, u32[]{:S(2)}, u32[]{:S(2)}) collective-permute-start(bf16[16,128]{1,0:T(8,128)(2,1)S(1)} %get-tuple-element.8), channel_id=1, source_target_pairs={{0,3},{1,2},{2,1},{3,0},{4,7},{5,6},{6,5},{7,4},{8,11},{9,10},{10,... | collective-permute-start | bytes 12296 | tf_op jit(solution)/shard_map/ppermute | solution.py:22
  5.5 1.2 %filters.1 = bf16[128,128]{1,0:T(8,128)(2,1)S(1)} custom-call(bf16[32,2048]{1,0:T(8,128)(2,1)} %bitcast.6, bf16[8,32]{1,0:T(8,128)(2,1)} %bitcast.11, s32[1]{0:T(128)S(6)} %copy.17.count), custom_call_target="tpu_custom_call" | custom-call | tf_op jit(solution)/shard_map/filters/pallas_call | solution.py:440
  6.7 0.0 collective-permute-done
  6.7 1.9 %collective-permute-start.1 = (bf16[160,128]{1,0:T(8,128)(2,1)S(1)}, bf16[160,128]{1,0:T(8,128)(2,1)S(1)}, u32[]{:S(2)}, u32[]{:S(2)}) collective-permute-start(bf16[160,128]{1,0:T(8,128)(2,1)S(1)} %pad_maximum_fusion.1), channel_id=1, source_target_pairs={{0,5},{1,4},{4,1},{5,0},{8,13},{9,12},{12,9},{13,8},{2,7},{3,6},{6... | collective-permute-start | bytes 122888 | tf_op jit(solution)/shard_map/ppermute | solution.py:22
  8.6 2.2 %collective-permute-start.2 = (bf16[160,128]{1,0:T(8,128)(2,1)S(1)}, bf16[160,128]{1,0:T(8,128)(2,1)S(1)}, u32[]{:S(2)}, u32[]{:S(2)}) collective-permute-start(bf16[160,128]{1,0:T(8,128)(2,1)S(1)} %pad_maximum_fusion.1), channel_id=1, source_target_pairs={{0,9},{1,8},{4,13},{5,12},{8,1},{9,0},{12,5},{13,4},{2,11},{3,10},... | collective-permute-start | bytes 122888 | tf_op jit(solution)/shard_map/ppermute | solution.py:22
  10.9 0.0 collective-permute-done.1
  10.9 0.5 %collective-permute-start.4 = (bf16[320,128]{1,0:T(8,128)(2,1)S(1)}, bf16[320,128]{1,0:T(8,128)(2,1)S(1)}, u32[]{:S(2)}, u32[]{:S(2)}) collective-permute-start(bf16[320,128]{1,0:T(8,128)(2,1)S(1)} %pad_maximum_fusion.own_a), channel_id=1, source_target_pairs={{0,1},{1,0},{2,3},{3,2},{4,5},{5,4},{6,7},{7,6},{8,9},{9,8},{10,11... | collective-permute-start | bytes 245768 | tf_op jit(solution)/shard_map/ppermute | solution.py:26
  11.4 2.7 %collective-permute-done.2 = bf16[160,128]{1,0:T(8,128)(2,1)S(1)} collective-permute-done((bf16[160,128]{1,0:T(8,128)(2,1)S(1)}, bf16[160,128]{1,0:T(8,128)(2,1)S(1)}, u32[]{:S(2)}, u32[]{:S(2)}) %collective-permute-start.2) | collective-permute-done | bytes 40992 | tf_op jit(solution)/shard_map/ppermute | solution.py:22
  14.1 0.0 collective-permute-start.3
  14.1 3.6 %collective-permute-done.3 = bf16[160,128]{1,0:T(8,128)(2,1)S(1)} collective-permute-done((bf16[160,128]{1,0:T(8,128)(2,1)S(1)}, bf16[160,128]{1,0:T(8,128)(2,1)S(1)}, u32[]{:S(2)}, u32[]{:S(2)}) %collective-permute-start.3) | collective-permute-done | bytes 40992 | tf_op jit(solution)/shard_map/ppermute | solution.py:22
  17.7 0.2 collective-permute-start.5
  17.9 0.4 %collective-permute-start.6 = (f32[8,128]{1,0:T(8,128)S(1)}, f32[8,128]{1,0:T(8,128)S(1)}, u32[]{:S(2)}, u32[]{:S(2)}) collective-permute-start(f32[8,128]{1,0:T(8,128)S(1)} %get-tuple-element.9.levels), channel_id=1, source_target_pairs={{0,1},{1,0},{2,3},{3,2},{4,5},{5,4},{6,7},{7,6},{8,9},{9,8},{10,11... | collective-permute-start | bytes 12296 | tf_op jit(solution)/shard_map/ppermute | solution.py:26
  18.3 0.8 %collective-permute-done.6.levels_other = f32[8,128]{1,0:T(8,128)S(1)} collective-permute-done((f32[8,128]{1,0:T(8,128)S(1)}, f32[8,128]{1,0:T(8,128)S(1)}, u32[]{:S(2)}, u32[]{:S(2)}) %collective-permute-start.6) | collective-permute-done | bytes 4128 | tf_op jit(solution)/shard_map/ppermute | solution.py:26
  19.1 0.0 copy-start.1
  19.1 1.3 %bands.1 = (bf16[4,3,256,128]{3,2,1,0:T(8,128)(2,1)S(1)}, bf16[4,3,256,128]{3,2,1,0:T(8,128)(2,1)S(1)}, f32[4,8,128]{2,1,0:T(8,128)S(1)}, f32[2,3,8,128]{3,2,1,0:T(8,128)S(1)}) custom-call(f32[4,2,257]{2,1,0:T(2,128)} %series.1, f32[8,128]{1,0:T(8,128)S(1)} %get-tuple-element.9.levels, f32[8,128]{1,0:T(8,128)S(1)} %collective-permute-done.6.levels_other), custom_call_target="tpu_custom_call" | custom-call | tf_op jit(solution)/shard_map/bands/pallas_call | solution.py:470
  20.4 0.0 collective-permute-done.4.other_a
  20.4 0.0 collective-permute-done.5.other_b
  20.4 0.0 copy-done
  20.4 0.0 copy-done.1
  20.4 2.3 %outputs.1 = (f32[4,2,1024]{2,1,0:T(2,128)}, f32[4,2,1024]{2,1,0:T(2,128)}) custom-call(bf16[320,128]{1,0:T(8,128)(2,1)S(1)} %pad_maximum_fusion.own_a, bf16[320,128]{1,0:T(8,128)(2,1)S(1)} %constant_dynamic-update-slice_fusion.own_b, bf16[320,128]{1,0:T(8,128)(2,1)S(1)} %collective-permute-done.4.other_a, ...), custom_call_target="tpu_custom_call" | custom-call | tf_op jit(solution)/shard_map/outputs/pallas_call | solution.py:487
  (4 shorter events, 0.0 us)
Async XLA Ops:
  0.6 19.8 %copy-start = (bf16[1024,256]{1,0:T(8,128)(2,1)S(1)}, bf16[1024,256]{1,0:T(8,128)(2,1)}, u32[]{:S(2)}) copy-start(bf16[1024,256]{1,0:T(8,128)(2,1)} %constant.11.clone.full) | copy-start | bytes 1572868
  2.4 4.3 %collective-permute-start = (bf16[16,128]{1,0:T(8,128)(2,1)S(1)}, bf16[16,128]{1,0:T(8,128)(2,1)S(1)}, u32[]{:S(2)}, u32[]{:S(2)}) collective-permute-start(bf16[16,128]{1,0:T(8,128)(2,1)S(1)} %get-tuple-element.8), channel_id=1, source_target_pairs={{0,3},{1,2},{2,1},{3,0},{4,7},{5,6},{6,5},{7,4},{8,11},{9,10},{10,... | collective-permute-start | bytes 12296 | tf_op jit(solution)/shard_map/ppermute | solution.py:22
  6.7 4.1 %collective-permute-start.1 = (bf16[160,128]{1,0:T(8,128)(2,1)S(1)}, bf16[160,128]{1,0:T(8,128)(2,1)S(1)}, u32[]{:S(2)}, u32[]{:S(2)}) collective-permute-start(bf16[160,128]{1,0:T(8,128)(2,1)S(1)} %pad_maximum_fusion.1), channel_id=1, source_target_pairs={{0,5},{1,4},{4,1},{5,0},{8,13},{9,12},{12,9},{13,8},{2,7},{3,6},{6... | collective-permute-start | bytes 122888 | tf_op jit(solution)/shard_map/ppermute | solution.py:22
  8.6 5.5 %collective-permute-start.2 = (bf16[160,128]{1,0:T(8,128)(2,1)S(1)}, bf16[160,128]{1,0:T(8,128)(2,1)S(1)}, u32[]{:S(2)}, u32[]{:S(2)}) collective-permute-start(bf16[160,128]{1,0:T(8,128)(2,1)S(1)} %pad_maximum_fusion.1), channel_id=1, source_target_pairs={{0,9},{1,8},{4,13},{5,12},{8,1},{9,0},{12,5},{13,4},{2,11},{3,10},... | collective-permute-start | bytes 122888 | tf_op jit(solution)/shard_map/ppermute | solution.py:22
  10.9 9.5 %collective-permute-start.4 = (bf16[320,128]{1,0:T(8,128)(2,1)S(1)}, bf16[320,128]{1,0:T(8,128)(2,1)S(1)}, u32[]{:S(2)}, u32[]{:S(2)}) collective-permute-start(bf16[320,128]{1,0:T(8,128)(2,1)S(1)} %pad_maximum_fusion.own_a), channel_id=1, source_target_pairs={{0,1},{1,0},{2,3},{3,2},{4,5},{5,4},{6,7},{7,6},{8,9},{9,8},{10,11... | collective-permute-start | bytes 245768 | tf_op jit(solution)/shard_map/ppermute | solution.py:26
  14.1 3.6 %collective-permute-start.3 = (bf16[160,128]{1,0:T(8,128)(2,1)S(1)}, bf16[160,128]{1,0:T(8,128)(2,1)S(1)}, u32[]{:S(2)}, u32[]{:S(2)}) collective-permute-start(bf16[160,128]{1,0:T(8,128)(2,1)S(1)} %collective-permute-done.2), channel_id=1, source_target_pairs={{0,5},{1,4},{4,1},{5,0},{8,13},{9,12},{12,9},{13,8},{2,7},{3,6},{6... | collective-permute-start | bytes 122888 | tf_op jit(solution)/shard_map/ppermute | solution.py:22
  17.7 2.7 %collective-permute-start.5 = (bf16[320,128]{1,0:T(8,128)(2,1)S(1)}, bf16[320,128]{1,0:T(8,128)(2,1)S(1)}, u32[]{:S(2)}, u32[]{:S(2)}) collective-permute-start(bf16[320,128]{1,0:T(8,128)(2,1)S(1)} %constant_dynamic-update-slice_fusion.own_b), channel_id=1, source_target_pairs={{0,1},{1,0},{2,3},{3,2},{4,5},{5,4},{6,7},{7,6},{8,9},{9,8},{10,11... | collective-permute-start | bytes 245768 | tf_op jit(solution)/shard_map/ppermute | solution.py:26
  17.9 1.2 %collective-permute-start.6 = (f32[8,128]{1,0:T(8,128)S(1)}, f32[8,128]{1,0:T(8,128)S(1)}, u32[]{:S(2)}, u32[]{:S(2)}) collective-permute-start(f32[8,128]{1,0:T(8,128)S(1)} %get-tuple-element.9.levels), channel_id=1, source_target_pairs={{0,1},{1,0},{2,3},{3,2},{4,5},{5,4},{6,7},{7,6},{8,9},{9,8},{10,11... | collective-permute-start | bytes 12296 | tf_op jit(solution)/shard_map/ppermute | solution.py:26
  19.1 1.3 %copy-start.1 = (f32[2,8,128]{2,1,0:T(8,128)S(1)}, f32[2,8,128]{2,1,0:T(8,128)}, u32[]{:S(2)}) copy-start(f32[2,8,128]{2,1,0:T(8,128)} %constant.8.clone.outer) | copy-start | bytes 24580

commit v6 on v5

--- a/solution.py
+++ b/solution.py
@@ -255,22 +255,28 @@
     first_t = first_out - (lags - 1)
     t_frames = lags - 1 + out_frames
     assert first_t == rows and first_t + t_frames - 1 == (near - 1) * rows
-    right = keep_right()
+    step = 16
+    u_row = lax.broadcasted_iota(jnp.int32, (step, LANES), 0)
+    q_lane = lax.broadcasted_iota(jnp.int32, (step, LANES), 1)
+    rights = [q_lane >= u_row + top for top in range(0, LANES, step)]
+
+    def turned(row):
+        whole = circulant(row).astype(BF16)
+        return [whole[top : top + step] for top in range(0, LANES, step)]
 
     def frame(c, s):
         at = c * (near - 1) * rows + (first_t + s) % ((near - 1) * rows)
-        return circulant(white[at : at + 1])
+        return turned(white[at : at + 1])
 
     earlier = [
-        circulant(white[top : top + 1])
-        for top in (first_t - 1, (near - 1) * rows + first_t - 1)
+        turned(white[top : top + 1]) for top in (first_t - 1, (near - 1) * rows + first_t - 1)
     ]
     toeplitz = []
     for s in range(t_frames):
         tiles = []
         for c in range(2):
             now = frame(c, s)
-            tiles.append(jnp.where(right, now, earlier[c]).astype(BF16))
+            tiles += [jnp.where(r, p, q) for r, p, q in zip(rights, now, earlier[c])]
             earlier[c] = now
         toeplitz.append(jnp.concatenate(tiles, axis=0))
 

time: 23 us -> 22.9 us (level)
  no operation moved by 1% of the time
where the time goes in v6:
time: 22.9 us; the launch traced here: 22.7 us
  starting transfers between devices  7.73 us (34%)
  waiting for transfers between devices  7.1 us (31%)
  Pallas kernels  5.74 us (25%)
  between operations  2.06 us (9%)
    ppermute x4, starting transfers between devices, swapped(): return lax.ppermute(block, (axis, 'rate'), route)  6.62 us
    ppermute x4, waiting for transfers between devices, swapped(): return lax.ppermute(block, (axis, 'rate'), route)  6.27 us
    pallas_call x1, Pallas kernels, body(): pl.pallas_call(functools.partial(output_kernel, slots=slots, tms=tms, len...  2.23 us
    pallas_call x1, Pallas kernels, body(): pl.pallas_call(band_kernel, out_shape=(band, band, pltpu.VMEM((banks, 8,...  1.29 us
    pallas_call x1, Pallas kernels, body(): pl.pallas_call(filter_kernel, out_shape=pltpu.VMEM((2 * templ * lags, LAN...  1.17 us
    ppermute x3, starting transfers between devices, swapped_cores(): lax.ppermute(block, 'rate', [(i, i ^ 1) for i in range(lax.axis_size('rat...  1.11 us
    pallas_call x1, Pallas kernels, body(): pl.pallas_call(spectrum_kernel, out_shape=(pltpu.VMEM((4 * high, LANES),...  1.04 us
    ppermute x3, waiting for transfers between devices, swapped_cores(): lax.ppermute(block, 'rate', [(i, i ^ 1) for i in range(lax.axis_size('rat...  0.83 us
  transfers between devices with their start and end apart: 7, of which 3 were waited for; matrix products, arithmetic and copies ran while one was open for 0% of the time, Pallas kernels for 11%

profile of v6, /device:TPU:0, one launch (start us, length us, event | category | flops | bytes accessed | tf_op | source)
XLA Modules:
  0.0 22.7 jit_solution(171479417236818570)
XLA Ops:
  0.6 0.0 copy-start
  1.3 1.0 %spectrum.1 = (bf16[16,128]{1,0:T(8,128)(2,1)S(1)}, f32[8,128]{1,0:T(8,128)S(1)}) custom-call(f32[8,128]{1,0:T(8,128)} %bitcast.7, s32[8,128]{1,0:T(8,128)} %bitcast.8, s32[1]{0:T(128)S(6)} %copy.16.reset, f32[4,128]{1,0:T(4,128)} %bitcast.9, f32[4,128]{1,0:T(4,128)} %bitcast.10, f32[2,8,128]{2,1,0:T(8,128)} %constant.8.clone.outer, ...), custom_call_target="tpu_custom_call" | custom-call | tf_op jit(solution)/shard_map/spectrum/pallas_call | solution.py:427
  2.4 2.5 %collective-permute-start = (bf16[16,128]{1,0:T(8,128)(2,1)S(1)}, bf16[16,128]{1,0:T(8,128)(2,1)S(1)}, u32[]{:S(2)}, u32[]{:S(2)}) collective-permute-start(bf16[16,128]{1,0:T(8,128)(2,1)S(1)} %get-tuple-element.8), channel_id=1, source_target_pairs={{0,3},{1,2},{2,1},{3,0},{4,7},{5,6},{6,5},{7,4},{8,11},{9,10},{10,... | collective-permute-start | bytes 12296 | tf_op jit(solution)/shard_map/ppermute | solution.py:22
  5.5 1.2 %filters.1 = bf16[128,128]{1,0:T(8,128)(2,1)S(1)} custom-call(bf16[32,2048]{1,0:T(8,128)(2,1)} %bitcast.6, bf16[8,32]{1,0:T(8,128)(2,1)} %bitcast.11, s32[1]{0:T(128)S(6)} %copy.17.count), custom_call_target="tpu_custom_call" | custom-call | tf_op jit(solution)/shard_map/filters/pallas_call | solution.py:446
  6.7 0.0 collective-permute-done
  6.7 1.9 %collective-permute-start.1 = (bf16[160,128]{1,0:T(8,128)(2,1)S(1)}, bf16[160,128]{1,0:T(8,128)(2,1)S(1)}, u32[]{:S(2)}, u32[]{:S(2)}) collective-permute-start(bf16[160,128]{1,0:T(8,128)(2,1)S(1)} %pad_maximum_fusion.1), channel_id=1, source_target_pairs={{0,5},{1,4},{4,1},{5,0},{8,13},{9,12},{12,9},{13,8},{2,7},{3,6},{6... | collective-permute-start | bytes 122888 | tf_op jit(solution)/shard_map/ppermute | solution.py:22
  8.6 2.2 %collective-permute-start.2 = (bf16[160,128]{1,0:T(8,128)(2,1)S(1)}, bf16[160,128]{1,0:T(8,128)(2,1)S(1)}, u32[]{:S(2)}, u32[]{:S(2)}) collective-permute-start(bf16[160,128]{1,0:T(8,128)(2,1)S(1)} %pad_maximum_fusion.1), channel_id=1, source_target_pairs={{0,9},{1,8},{4,13},{5,12},{8,1},{9,0},{12,5},{13,4},{2,11},{3,10},... | collective-permute-start | bytes 122888 | tf_op jit(solution)/shard_map/ppermute | solution.py:22
  10.9 0.0 collective-permute-done.1
  10.9 0.5 %collective-permute-start.4 = (bf16[320,128]{1,0:T(8,128)(2,1)S(1)}, bf16[320,128]{1,0:T(8,128)(2,1)S(1)}, u32[]{:S(2)}, u32[]{:S(2)}) collective-permute-start(bf16[320,128]{1,0:T(8,128)(2,1)S(1)} %pad_maximum_fusion.own_a), channel_id=1, source_target_pairs={{0,1},{1,0},{2,3},{3,2},{4,5},{5,4},{6,7},{7,6},{8,9},{9,8},{10,11... | collective-permute-start | bytes 245768 | tf_op jit(solution)/shard_map/ppermute | solution.py:26
  11.4 2.7 %collective-permute-done.2 = bf16[160,128]{1,0:T(8,128)(2,1)S(1)} collective-permute-done((bf16[160,128]{1,0:T(8,128)(2,1)S(1)}, bf16[160,128]{1,0:T(8,128)(2,1)S(1)}, u32[]{:S(2)}, u32[]{:S(2)}) %collective-permute-start.2) | collective-permute-done | bytes 40992 | tf_op jit(solution)/shard_map/ppermute | solution.py:22
  14.1 0.0 collective-permute-start.3
  14.1 3.6 %collective-permute-done.3 = bf16[160,128]{1,0:T(8,128)(2,1)S(1)} collective-permute-done((bf16[160,128]{1,0:T(8,128)(2,1)S(1)}, bf16[160,128]{1,0:T(8,128)(2,1)S(1)}, u32[]{:S(2)}, u32[]{:S(2)}) %collective-permute-start.3) | collective-permute-done | bytes 40992 | tf_op jit(solution)/shard_map/ppermute | solution.py:22
  17.7 0.2 collective-permute-start.5
  17.9 0.4 %collective-permute-start.6 = (f32[8,128]{1,0:T(8,128)S(1)}, f32[8,128]{1,0:T(8,128)S(1)}, u32[]{:S(2)}, u32[]{:S(2)}) collective-permute-start(f32[8,128]{1,0:T(8,128)S(1)} %get-tuple-element.9.levels), channel_id=1, source_target_pairs={{0,1},{1,0},{2,3},{3,2},{4,5},{5,4},{6,7},{7,6},{8,9},{9,8},{10,11... | collective-permute-start | bytes 12296 | tf_op jit(solution)/shard_map/ppermute | solution.py:26
  18.3 0.8 %collective-permute-done.6.levels_other = f32[8,128]{1,0:T(8,128)S(1)} collective-permute-done((f32[8,128]{1,0:T(8,128)S(1)}, f32[8,128]{1,0:T(8,128)S(1)}, u32[]{:S(2)}, u32[]{:S(2)}) %collective-permute-start.6) | collective-permute-done | bytes 4128 | tf_op jit(solution)/shard_map/ppermute | solution.py:26
  19.1 0.0 copy-start.1
  19.1 1.3 %bands.1 = (bf16[4,3,256,128]{3,2,1,0:T(8,128)(2,1)S(1)}, bf16[4,3,256,128]{3,2,1,0:T(8,128)(2,1)S(1)}, f32[4,8,128]{2,1,0:T(8,128)S(1)}, f32[2,3,8,128]{3,2,1,0:T(8,128)S(1)}) custom-call(f32[4,2,257]{2,1,0:T(2,128)} %series.1, f32[8,128]{1,0:T(8,128)S(1)} %get-tuple-element.9.levels, f32[8,128]{1,0:T(8,128)S(1)} %collective-permute-done.6.levels_other), custom_call_target="tpu_custom_call" | custom-call | tf_op jit(solution)/shard_map/bands/pallas_call | solution.py:476
  20.4 0.0 collective-permute-done.4.other_a
  20.4 0.0 collective-permute-done.5.other_b
  20.4 0.0 copy-done
  20.4 0.0 copy-done.1
  20.4 2.2 %outputs.1 = (f32[4,2,1024]{2,1,0:T(2,128)}, f32[4,2,1024]{2,1,0:T(2,128)}) custom-call(bf16[320,128]{1,0:T(8,128)(2,1)S(1)} %pad_maximum_fusion.own_a, bf16[320,128]{1,0:T(8,128)(2,1)S(1)} %constant_dynamic-update-slice_fusion.own_b, bf16[320,128]{1,0:T(8,128)(2,1)S(1)} %collective-permute-done.4.other_a, ...), custom_call_target="tpu_custom_call" | custom-call | tf_op jit(solution)/shard_map/outputs/pallas_call | solution.py:493
  (4 shorter events, 0.0 us)
Async XLA Ops:
  0.6 19.8 %copy-start = (bf16[1024,256]{1,0:T(8,128)(2,1)S(1)}, bf16[1024,256]{1,0:T(8,128)(2,1)}, u32[]{:S(2)}) copy-start(bf16[1024,256]{1,0:T(8,128)(2,1)} %constant.11.clone.full) | copy-start | bytes 1572868
  2.4 4.3 %collective-permute-start = (bf16[16,128]{1,0:T(8,128)(2,1)S(1)}, bf16[16,128]{1,0:T(8,128)(2,1)S(1)}, u32[]{:S(2)}, u32[]{:S(2)}) collective-permute-start(bf16[16,128]{1,0:T(8,128)(2,1)S(1)} %get-tuple-element.8), channel_id=1, source_target_pairs={{0,3},{1,2},{2,1},{3,0},{4,7},{5,6},{6,5},{7,4},{8,11},{9,10},{10,... | collective-permute-start | bytes 12296 | tf_op jit(solution)/shard_map/ppermute | solution.py:22
  6.7 4.1 %collective-permute-start.1 = (bf16[160,128]{1,0:T(8,128)(2,1)S(1)}, bf16[160,128]{1,0:T(8,128)(2,1)S(1)}, u32[]{:S(2)}, u32[]{:S(2)}) collective-permute-start(bf16[160,128]{1,0:T(8,128)(2,1)S(1)} %pad_maximum_fusion.1), channel_id=1, source_target_pairs={{0,5},{1,4},{4,1},{5,0},{8,13},{9,12},{12,9},{13,8},{2,7},{3,6},{6... | collective-permute-start | bytes 122888 | tf_op jit(solution)/shard_map/ppermute | solution.py:22
  8.6 5.5 %collective-permute-start.2 = (bf16[160,128]{1,0:T(8,128)(2,1)S(1)}, bf16[160,128]{1,0:T(8,128)(2,1)S(1)}, u32[]{:S(2)}, u32[]{:S(2)}) collective-permute-start(bf16[160,128]{1,0:T(8,128)(2,1)S(1)} %pad_maximum_fusion.1), channel_id=1, source_target_pairs={{0,9},{1,8},{4,13},{5,12},{8,1},{9,0},{12,5},{13,4},{2,11},{3,10},... | collective-permute-start | bytes 122888 | tf_op jit(solution)/shard_map/ppermute | solution.py:22
  10.9 9.5 %collective-permute-start.4 = (bf16[320,128]{1,0:T(8,128)(2,1)S(1)}, bf16[320,128]{1,0:T(8,128)(2,1)S(1)}, u32[]{:S(2)}, u32[]{:S(2)}) collective-permute-start(bf16[320,128]{1,0:T(8,128)(2,1)S(1)} %pad_maximum_fusion.own_a), channel_id=1, source_target_pairs={{0,1},{1,0},{2,3},{3,2},{4,5},{5,4},{6,7},{7,6},{8,9},{9,8},{10,11... | collective-permute-start | bytes 245768 | tf_op jit(solution)/shard_map/ppermute | solution.py:26
  14.1 3.6 %collective-permute-start.3 = (bf16[160,128]{1,0:T(8,128)(2,1)S(1)}, bf16[160,128]{1,0:T(8,128)(2,1)S(1)}, u32[]{:S(2)}, u32[]{:S(2)}) collective-permute-start(bf16[160,128]{1,0:T(8,128)(2,1)S(1)} %collective-permute-done.2), channel_id=1, source_target_pairs={{0,5},{1,4},{4,1},{5,0},{8,13},{9,12},{12,9},{13,8},{2,7},{3,6},{6... | collective-permute-start | bytes 122888 | tf_op jit(solution)/shard_map/ppermute | solution.py:22
  17.7 2.7 %collective-permute-start.5 = (bf16[320,128]{1,0:T(8,128)(2,1)S(1)}, bf16[320,128]{1,0:T(8,128)(2,1)S(1)}, u32[]{:S(2)}, u32[]{:S(2)}) collective-permute-start(bf16[320,128]{1,0:T(8,128)(2,1)S(1)} %constant_dynamic-update-slice_fusion.own_b), channel_id=1, source_target_pairs={{0,1},{1,0},{2,3},{3,2},{4,5},{5,4},{6,7},{7,6},{8,9},{9,8},{10,11... | collective-permute-start | bytes 245768 | tf_op jit(solution)/shard_map/ppermute | solution.py:26
  17.9 1.2 %collective-permute-start.6 = (f32[8,128]{1,0:T(8,128)S(1)}, f32[8,128]{1,0:T(8,128)S(1)}, u32[]{:S(2)}, u32[]{:S(2)}) collective-permute-start(f32[8,128]{1,0:T(8,128)S(1)} %get-tuple-element.9.levels), channel_id=1, source_target_pairs={{0,1},{1,0},{2,3},{3,2},{4,5},{5,4},{6,7},{7,6},{8,9},{9,8},{10,11... | collective-permute-start | bytes 12296 | tf_op jit(solution)/shard_map/ppermute | solution.py:26
  19.1 1.3 %copy-start.1 = (f32[2,8,128]{2,1,0:T(8,128)S(1)}, f32[2,8,128]{2,1,0:T(8,128)}, u32[]{:S(2)}) copy-start(f32[2,8,128]{2,1,0:T(8,128)} %constant.8.clone.outer) | copy-start | bytes 24580

commit v7 on v6

--- a/solution.py
+++ b/solution.py
@@ -175,14 +175,14 @@
     behind = -(-(taps + window) // length)
     near = behind + 2
     banks = len(slots)
-    half = banks // 2
+    whole = banks - banks // 4
     bank = lax.axis_index("bank")
     tm = lax.axis_index("tm")
     place = bank * tms + tm
     bufs = ((own_a, own_b), (other_a, other_b))
 
     def piece(c, d):
-        return bufs[c][d // half], (d % half) * piece_rows
+        return bufs[c][d // whole], d % whole * piece_rows
 
     tile_row = lax.broadcasted_iota(jnp.int32, (2 * high, LANES), 0)
     tile_lane = lax.broadcasted_iota(jnp.int32, (2 * high, LANES), 1)
@@ -463,14 +463,13 @@
         distance //= 2
     far = swapped(held, "bank", 2)
     near = swapped(held, "bank", 1)
-    first = jnp.concatenate([held, near])
     levels_other = swapped_cores(levels)
     last = swapped(far, "bank", 1)
-    second = jnp.concatenate([far, last])
+    early = jnp.concatenate([held, near, far])
     slots = slots + [(d ^ 1, p ^ 1) for d, p in slots]
     slots = slots + [(d ^ 2, p ^ 1) for d, p in slots]
-    first_other = swapped_cores(first)
-    second_other = swapped_cores(second)
+    early_other = swapped_cores(early)
+    last_other = swapped_cores(last)
 
     band = on_chip_shape((banks, 3, 2 * LANES, LANES), BF16)
     band_up, band_low, lag, levels = pl.pallas_call(
@@ -504,7 +503,7 @@
             pltpu.VMEM((2, banks * tms + behind + 1, 2 * high, LANES), F32),
         ],
         name="outputs",
-    )(*on_chip(first, second, first_other, second_other, full, outer, band_up, band_low, lag, levels))
+    )(*on_chip(early, last, early_other, last_other, full, outer, band_up, band_low, lag, levels))
 
 
 def solution(mesh):

time: 22.9 us -> 22.3 us (0.974)
  waiting for transfers between devices: 7.1 us -> 5.34 us
  starting transfers between devices: 7.73 us -> 8.88 us
    ppermute x4, waiting for transfers between devices: 6.27 us -> 4.29 us  [swapped(): return lax.ppermute(block, (axis, 'rate'), route)]
    ppermute x4, starting transfers between devices: 6.62 us -> 8.19 us  [swapped(): return lax.ppermute(block, (axis, 'rate'), route)]
    ppermute x3, starting transfers between devices: 1.11 us -> 0.69 us  [swapped_cores(): lax.ppermute(block, 'rate', [(i, i ^ 1) for i in range(lax.axis_size('rat...]
where the time goes in v7:
time: 22.3 us; the launch traced here: 22.1 us
  starting transfers between devices  8.88 us (40%)
  Pallas kernels  5.74 us (26%)
  waiting for transfers between devices  5.34 us (24%)
  between operations  2.06 us (9%)
    ppermute x4, starting transfers between devices, swapped(): return lax.ppermute(block, (axis, 'rate'), route)  8.19 us
    ppermute x4, waiting for transfers between devices, swapped(): return lax.ppermute(block, (axis, 'rate'), route)  4.29 us
    pallas_call x1, Pallas kernels, body(): pl.pallas_call(functools.partial(output_kernel, slots=slots, tms=tms, len...  2.23 us
    pallas_call x1, Pallas kernels, body(): pl.pallas_call(band_kernel, out_shape=(band, band, pltpu.VMEM((banks, 8,...  1.29 us
    pallas_call x1, Pallas kernels, body(): pl.pallas_call(filter_kernel, out_shape=pltpu.VMEM((2 * templ * lags, LAN...  1.17 us
    ppermute x3, waiting for transfers between devices, swapped_cores(): lax.ppermute(block, 'rate', [(i, i ^ 1) for i in range(lax.axis_size('rat...  1.06 us
    pallas_call x1, Pallas kernels, body(): pl.pallas_call(spectrum_kernel, out_shape=(pltpu.VMEM((4 * high, LANES),...  1.04 us
    ppermute x3, starting transfers between devices, swapped_cores(): lax.ppermute(block, 'rate', [(i, i ^ 1) for i in range(lax.axis_size('rat...  0.69 us
  transfers between devices with their start and end apart: 7, of which 3 were waited for; matrix products, arithmetic and copies ran while one was open for 0% of the time, Pallas kernels for 11%

profile of v7, /device:TPU:0, one launch (start us, length us, event | category | flops | bytes accessed | tf_op | source)
XLA Modules:
  0.0 22.1 jit_solution(5407675482465362851)
XLA Ops:
  0.6 0.0 copy-start
  1.3 1.0 %spectrum.1 = (bf16[16,128]{1,0:T(8,128)(2,1)S(1)}, f32[8,128]{1,0:T(8,128)S(1)}) custom-call(f32[8,128]{1,0:T(8,128)} %bitcast.7, s32[8,128]{1,0:T(8,128)} %bitcast.8, s32[1]{0:T(128)S(6)} %copy.19.reset, f32[4,128]{1,0:T(4,128)} %bitcast.9, f32[4,128]{1,0:T(4,128)} %bitcast.10, f32[2,8,128]{2,1,0:T(8,128)} %constant.8.clone.outer, ...), custom_call_target="tpu_custom_call" | custom-call | tf_op jit(solution)/shard_map/spectrum/pallas_call | solution.py:427
  2.4 2.5 %collective-permute-start = (bf16[16,128]{1,0:T(8,128)(2,1)S(1)}, bf16[16,128]{1,0:T(8,128)(2,1)S(1)}, u32[]{:S(2)}, u32[]{:S(2)}) collective-permute-start(bf16[16,128]{1,0:T(8,128)(2,1)S(1)} %get-tuple-element.8), channel_id=1, source_target_pairs={{0,3},{1,2},{2,1},{3,0},{4,7},{5,6},{6,5},{7,4},{8,11},{9,10},{10,... | collective-permute-start | bytes 12296 | tf_op jit(solution)/shard_map/ppermute | solution.py:22
  5.5 1.2 %filters.1 = bf16[128,128]{1,0:T(8,128)(2,1)S(1)} custom-call(bf16[32,2048]{1,0:T(8,128)(2,1)} %bitcast.6, bf16[8,32]{1,0:T(8,128)(2,1)} %bitcast.11, s32[1]{0:T(128)S(6)} %copy.20.count), custom_call_target="tpu_custom_call" | custom-call | tf_op jit(solution)/shard_map/filters/pallas_call | solution.py:446
  6.7 0.0 collective-permute-done
  6.7 2.9 %collective-permute-start.2 = (bf16[160,128]{1,0:T(8,128)(2,1)S(1)}, bf16[160,128]{1,0:T(8,128)(2,1)S(1)}, u32[]{:S(2)}, u32[]{:S(2)}) collective-permute-start(bf16[160,128]{1,0:T(8,128)(2,1)S(1)} %pad_maximum_fusion), channel_id=1, source_target_pairs={{0,9},{1,8},{4,13},{5,12},{8,1},{9,0},{12,5},{13,4},{2,11},{3,10},... | collective-permute-start | bytes 122888 | tf_op jit(solution)/shard_map/ppermute | solution.py:22
  9.6 1.2 %collective-permute-start.1 = (bf16[160,128]{1,0:T(8,128)(2,1)S(1)}, bf16[160,128]{1,0:T(8,128)(2,1)S(1)}, u32[]{:S(2)}, u32[]{:S(2)}) collective-permute-start(bf16[160,128]{1,0:T(8,128)(2,1)S(1)} %pad_maximum_fusion), channel_id=1, source_target_pairs={{0,5},{1,4},{4,1},{5,0},{8,13},{9,12},{12,9},{13,8},{2,7},{3,6},{6... | collective-permute-start | bytes 122888 | tf_op jit(solution)/shard_map/ppermute | solution.py:22
  10.9 2.4 %collective-permute-done.1 = bf16[160,128]{1,0:T(8,128)(2,1)S(1)} collective-permute-done((bf16[160,128]{1,0:T(8,128)(2,1)S(1)}, bf16[160,128]{1,0:T(8,128)(2,1)S(1)}, u32[]{:S(2)}, u32[]{:S(2)}) %collective-permute-start.1) | collective-permute-done | bytes 40992 | tf_op jit(solution)/shard_map/ppermute | solution.py:22
  13.3 0.0 collective-permute-done.2
  13.3 0.2 collective-permute-start.4
  13.5 1.6 %collective-permute-start.3 = (bf16[160,128]{1,0:T(8,128)(2,1)S(1)}, bf16[160,128]{1,0:T(8,128)(2,1)S(1)}, u32[]{:S(2)}, u32[]{:S(2)}) collective-permute-start(bf16[160,128]{1,0:T(8,128)(2,1)S(1)} %collective-permute-done.2), channel_id=1, source_target_pairs={{0,5},{1,4},{4,1},{5,0},{8,13},{9,12},{12,9},{13,8},{2,7},{3,6},{6... | collective-permute-start | bytes 122888 | tf_op jit(solution)/shard_map/ppermute | solution.py:22
  15.1 1.9 %collective-permute-done.3.own_b = bf16[160,128]{1,0:T(8,128)(2,1)S(1)} collective-permute-done((bf16[160,128]{1,0:T(8,128)(2,1)S(1)}, bf16[160,128]{1,0:T(8,128)(2,1)S(1)}, u32[]{:S(2)}, u32[]{:S(2)}) %collective-permute-start.3) | collective-permute-done | bytes 40992 | tf_op jit(solution)/shard_map/ppermute | solution.py:22
  16.9 0.4 %collective-permute-start.5 = (bf16[160,128]{1,0:T(8,128)(2,1)S(1)}, bf16[160,128]{1,0:T(8,128)(2,1)S(1)}, u32[]{:S(2)}, u32[]{:S(2)}) collective-permute-start(bf16[160,128]{1,0:T(8,128)(2,1)S(1)} %collective-permute-done.3.own_b), channel_id=1, source_target_pairs={{0,1},{1,0},{2,3},{3,2},{4,5},{5,4},{6,7},{7,6},{8,9},{9,8},{10,11... | collective-permute-start | bytes 122888 | tf_op jit(solution)/shard_map/ppermute | solution.py:26
  17.3 0.1 collective-permute-start.6
  17.5 1.1 %collective-permute-done.6.levels_other = f32[8,128]{1,0:T(8,128)S(1)} collective-permute-done((f32[8,128]{1,0:T(8,128)S(1)}, f32[8,128]{1,0:T(8,128)S(1)}, u32[]{:S(2)}, u32[]{:S(2)}) %collective-permute-start.6) | collective-permute-done | bytes 4128 | tf_op jit(solution)/shard_map/ppermute | solution.py:26
  18.5 0.0 copy-start.1
  18.5 1.3 %bands.1 = (bf16[4,3,256,128]{3,2,1,0:T(8,128)(2,1)S(1)}, bf16[4,3,256,128]{3,2,1,0:T(8,128)(2,1)S(1)}, f32[4,8,128]{2,1,0:T(8,128)S(1)}, f32[2,3,8,128]{3,2,1,0:T(8,128)S(1)}) custom-call(f32[4,2,257]{2,1,0:T(2,128)} %series.1, f32[8,128]{1,0:T(8,128)S(1)} %get-tuple-element.9.levels, f32[8,128]{1,0:T(8,128)S(1)} %collective-permute-done.6.levels_other), custom_call_target="tpu_custom_call" | custom-call | tf_op jit(solution)/shard_map/bands/pallas_call | solution.py:475
  19.8 0.0 collective-permute-done.5.other_b
  19.8 0.0 collective-permute-done.4.other_a
  19.8 0.0 copy-done
  19.8 0.0 copy-done.1
  19.9 2.2 %outputs.1 = (f32[4,2,1024]{2,1,0:T(2,128)}, f32[4,2,1024]{2,1,0:T(2,128)}) custom-call(bf16[480,128]{1,0:T(8,128)(2,1)S(1)} %constant_dynamic-update-slice_fusion.own_a, bf16[160,128]{1,0:T(8,128)(2,1)S(1)} %collective-permute-done.3.own_b, bf16[480,128]{1,0:T(8,128)(2,1)S(1)} %collective-permute-done.4.other_a, ...), custom_call_target="tpu_custom_call" | custom-call | tf_op jit(solution)/shard_map/outputs/pallas_call | solution.py:492
  (6 shorter events, 0.0 us)
Async XLA Ops:
  0.6 19.2 %copy-start = (bf16[1024,256]{1,0:T(8,128)(2,1)S(1)}, bf16[1024,256]{1,0:T(8,128)(2,1)}, u32[]{:S(2)}) copy-start(bf16[1024,256]{1,0:T(8,128)(2,1)} %constant.11.clone.full) | copy-start | bytes 1572868
  2.4 4.3 %collective-permute-start = (bf16[16,128]{1,0:T(8,128)(2,1)S(1)}, bf16[16,128]{1,0:T(8,128)(2,1)S(1)}, u32[]{:S(2)}, u32[]{:S(2)}) collective-permute-start(bf16[16,128]{1,0:T(8,128)(2,1)S(1)} %get-tuple-element.8), channel_id=1, source_target_pairs={{0,3},{1,2},{2,1},{3,0},{4,7},{5,6},{6,5},{7,4},{8,11},{9,10},{10,... | collective-permute-start | bytes 12296 | tf_op jit(solution)/shard_map/ppermute | solution.py:22
  6.7 6.6 %collective-permute-start.2 = (bf16[160,128]{1,0:T(8,128)(2,1)S(1)}, bf16[160,128]{1,0:T(8,128)(2,1)S(1)}, u32[]{:S(2)}, u32[]{:S(2)}) collective-permute-start(bf16[160,128]{1,0:T(8,128)(2,1)S(1)} %pad_maximum_fusion), channel_id=1, source_target_pairs={{0,9},{1,8},{4,13},{5,12},{8,1},{9,0},{12,5},{13,4},{2,11},{3,10},... | collective-permute-start | bytes 122888 | tf_op jit(solution)/shard_map/ppermute | solution.py:22
  9.6 3.7 %collective-permute-start.1 = (bf16[160,128]{1,0:T(8,128)(2,1)S(1)}, bf16[160,128]{1,0:T(8,128)(2,1)S(1)}, u32[]{:S(2)}, u32[]{:S(2)}) collective-permute-start(bf16[160,128]{1,0:T(8,128)(2,1)S(1)} %pad_maximum_fusion), channel_id=1, source_target_pairs={{0,5},{1,4},{4,1},{5,0},{8,13},{9,12},{12,9},{13,8},{2,7},{3,6},{6... | collective-permute-start | bytes 122888 | tf_op jit(solution)/shard_map/ppermute | solution.py:22
  13.3 6.5 %collective-permute-start.4 = (bf16[480,128]{1,0:T(8,128)(2,1)S(1)}, bf16[480,128]{1,0:T(8,128)(2,1)S(1)}, u32[]{:S(2)}, u32[]{:S(2)}) collective-permute-start(bf16[480,128]{1,0:T(8,128)(2,1)S(1)} %constant_dynamic-update-slice_fusion.own_a), channel_id=1, source_target_pairs={{0,1},{1,0},{2,3},{3,2},{4,5},{5,4},{6,7},{7,6},{8,9},{9,8},{10,11... | collective-permute-start | bytes 368648 | tf_op jit(solution)/shard_map/ppermute | solution.py:26
  13.5 3.4 %collective-permute-start.3 = (bf16[160,128]{1,0:T(8,128)(2,1)S(1)}, bf16[160,128]{1,0:T(8,128)(2,1)S(1)}, u32[]{:S(2)}, u32[]{:S(2)}) collective-permute-start(bf16[160,128]{1,0:T(8,128)(2,1)S(1)} %collective-permute-done.2), channel_id=1, source_target_pairs={{0,5},{1,4},{4,1},{5,0},{8,13},{9,12},{12,9},{13,8},{2,7},{3,6},{6... | collective-permute-start | bytes 122888 | tf_op jit(solution)/shard_map/ppermute | solution.py:22
  16.9 2.9 %collective-permute-start.5 = (bf16[160,128]{1,0:T(8,128)(2,1)S(1)}, bf16[160,128]{1,0:T(8,128)(2,1)S(1)}, u32[]{:S(2)}, u32[]{:S(2)}) collective-permute-start(bf16[160,128]{1,0:T(8,128)(2,1)S(1)} %collective-permute-done.3.own_b), channel_id=1, source_target_pairs={{0,1},{1,0},{2,3},{3,2},{4,5},{5,4},{6,7},{7,6},{8,9},{9,8},{10,11... | collective-permute-start | bytes 122888 | tf_op jit(solution)/shard_map/ppermute | solution.py:26
  17.3 1.2 %collective-permute-start.6 = (f32[8,128]{1,0:T(8,128)S(1)}, f32[8,128]{1,0:T(8,128)S(1)}, u32[]{:S(2)}, u32[]{:S(2)}) collective-permute-start(f32[8,128]{1,0:T(8,128)S(1)} %get-tuple-element.9.levels), channel_id=1, source_target_pairs={{0,1},{1,0},{2,3},{3,2},{4,5},{5,4},{6,7},{7,6},{8,9},{9,8},{10,11... | collective-permute-start | bytes 12296 | tf_op jit(solution)/shard_map/ppermute | solution.py:26
  18.5 1.3 %copy-start.1 = (f32[2,8,128]{2,1,0:T(8,128)S(1)}, f32[2,8,128]{2,1,0:T(8,128)}, u32[]{:S(2)}) copy-start(f32[2,8,128]{2,1,0:T(8,128)} %constant.8.clone.outer) | copy-start | bytes 24580
